TPU v7x, 128 devices: a whole 4x4x4 slice. The times are simulated.
128 devices in a mesh: row: 8 (over x, core), col: 16 (over y, z).
Axes of the slice: x: 4, y: 4, z: 4, core: 2. Of those that a mesh axis runs over, the one named last changes fastest.
Arguments:
- front_block: bfloat16 [16384, 16384], P('row', 'col'), may hold values from -0.046875 to 0.046875
- probe_right: bfloat16 [16384, 256], P('col'), may hold values from -6 to 6
- probe_left: bfloat16 [16384, 256], P('row'), may hold values from -6 to 6
- row_leaf: int32 [16384, 1], replicated, may hold values from 0 to 127; in each aligned block of 128 rows (0 to 127, 128 to 255, ...) at most 2 rows name the same one
- tree_leaf: int32 [128], replicated, may hold values from 0 to 127, each once
Outputs:
- coupling: float32 [128, 256, 256], P(('row', 'col'))
- merged: float32 [128, 256, 256], P(('row', 'col'))
Inputs may be any that keep to these rules, and one draw needn't show every extreme that they name: `row_leaf`: in each aligned block of 128 rows no leaf is named by more than 2 rows, a bound that some block reaches; every leaf has one row or more. `tree_leaf`: each leaf once. Positions that differ in bit 0 are siblings; their parents, at positions differing in bit 1, are siblings at the next level.
All inputs are finite; a program needn't handle non-finite values.
Results may differ from a plain program's by a relative error of at most 0.0092.
Values may be sent and summed in bfloat16 or wider, within the bound.
A program may use at most 64 MiB of HBM per device.

v0:
```python
import jax
import jax.numpy as jnp
from jax import lax
from jax.sharding import PartitionSpec as P

eps = 1e-05


def from_partner(value, axis, distance):
    mask = 2**distance
    pairs = [(source, source ^ mask) for source in range(lax.axis_size(axis))]
    return lax.ppermute(value, axis, pairs)


def exact_dot(left, right):
    return jnp.dot(left, right, precision=lax.Precision.HIGHEST, preferred_element_type=jnp.float32)


def whiten_cross(gram_sum, squares, cross_sum):
    width = gram_sum.shape[0]
    ridge = squares / width + eps
    factor = jnp.linalg.cholesky(gram_sum + ridge * jnp.eye(width, dtype=jnp.float32))
    return lax.linalg.triangular_solve(factor, cross_sum, left_side=True, lower=True)


def merge_pair(mine, other):
    gram_sum = exact_dot(mine.T, mine) + exact_dot(other.T, other)
    squares = jnp.sum(mine * mine) + jnp.sum(other * other)
    cross_sum = exact_dot(mine.T, other) + exact_dot(other.T, mine)
    return whiten_cross(gram_sum, squares, cross_sum)


def route_rows(rows, leaves, places, block_index, rows_dev, capacity, devices):
    block_leaf = lax.dynamic_slice_in_dim(leaves, block_index * rows_dev, rows_dev)
    positions = jnp.arange(devices, dtype=jnp.int32)
    owner_pos = jnp.sum(
        jnp.where(block_leaf[:, None] == positions[None, :], places[None, :], 0), axis=1
    )
    order_ids = jnp.arange(rows_dev, dtype=jnp.int32)
    earlier = (owner_pos[:, None] == owner_pos[None, :]) & (order_ids[None, :] < order_ids[:, None])
    rank_in = jnp.sum(earlier.astype(jnp.int32), axis=1)
    slot_index = owner_pos * capacity + rank_in
    buffer = jnp.zeros((devices * capacity, rows.shape[1]), rows.dtype)
    return buffer.at[slot_index].set(rows)


def per_device(front_block, probe_right, probe_left, row_leaf, tree_leaf):
    row_count = lax.axis_size("row")
    col_count = lax.axis_size("col")
    devices = row_count * col_count
    row_index = lax.axis_index("row")
    col_index = lax.axis_index("col")
    tile_rows, tile_cols = front_block.shape
    samples = probe_right.shape[1]
    leaves = row_leaf[:, 0]
    total_rows = leaves.shape[0]
    rows_dev = total_rows // devices
    capacity = max(2, 2 * rows_dev // devices)
    contract = (((0,), (0,)), ((), ()))
    rows_leaf = lax.dynamic_slice_in_dim(leaves, row_index * tile_rows, tile_rows)
    cols_leaf = lax.dynamic_slice_in_dim(leaves, col_index * tile_cols, tile_cols)
    same_leaf = rows_leaf[:, None] == cols_leaf[None, :]
    masked = jnp.where(same_leaf, front_block, jnp.zeros_like(front_block))
    forward_full = jnp.dot(front_block, probe_right, preferred_element_type=jnp.float32)
    forward_diag = jnp.dot(masked, probe_right, preferred_element_type=jnp.float32)
    backward_full = lax.dot_general(
        front_block, probe_left, contract, preferred_element_type=jnp.float32
    )
    backward_diag = lax.dot_general(
        masked, probe_left, contract, preferred_element_type=jnp.float32
    )
    forward_sum, forward_diag_sum = (
        lax.psum_scatter(forward_full, "col", scatter_dimension=0, tiled=True),
        lax.psum_scatter(forward_diag, "col", scatter_dimension=0, tiled=True),
    )
    backward_sum, backward_diag_sum = (
        lax.psum_scatter(backward_full, "row", scatter_dimension=0, tiled=True),
        lax.psum_scatter(backward_diag, "row", scatter_dimension=0, tiled=True),
    )
    forward = forward_sum - forward_diag_sum
    backward = backward_sum - backward_diag_sum
    sample_rows = forward.astype(jnp.bfloat16)
    sample_back = backward.astype(jnp.bfloat16)
    positions = jnp.arange(devices, dtype=jnp.int32)
    places = jnp.sum(
        jnp.where(tree_leaf[:, None] == positions[None, :], positions[:, None], 0), axis=0
    )
    forward_block = row_index * col_count + col_index
    backward_block = col_index * row_count + row_index
    forward_send = route_rows(
        sample_rows, leaves, places, forward_block, rows_dev, capacity, devices
    )
    backward_send = route_rows(
        sample_back, leaves, places, backward_block, rows_dev, capacity, devices
    )
    forward_recv, backward_recv = (
        lax.all_to_all(forward_send, ("row", "col"), split_axis=0, concat_axis=0, tiled=True),
        lax.all_to_all(backward_send, ("row", "col"), split_axis=0, concat_axis=0, tiled=True),
    )
    gram_sum = lax.dot_general(
        forward_recv, forward_recv, contract, preferred_element_type=jnp.float32
    )
    wide_rows = forward_recv.astype(jnp.float32)
    squares = jnp.sum(wide_rows * wide_rows)
    forward_grid = forward_recv.reshape(col_count, row_count, capacity, samples)
    backward_grid = backward_recv.reshape(row_count, col_count, capacity, samples)
    cross_sum = jnp.einsum(
        "jikr,ijks->rs", forward_grid, backward_grid, preferred_element_type=jnp.float32
    )
    coupling = whiten_cross(gram_sum, squares, cross_sum)
    merged = coupling
    for depth_level in range(2):
        partner = from_partner(merged, "col", depth_level)
        merged = merge_pair(merged, partner)
    return (coupling[None], merged[None])


def solution(mesh):
    return jax.shard_map(
        per_device,
        mesh=mesh,
        in_specs=(P("row", "col"), P("col", None), P("row", None), P(), P()),
        out_specs=(P(("row", "col"), None, None), P(("row", "col"), None, None)),
        check_vma=False,
    )
```

profile of v0, /device:TPU:1, one launch (start us, length us, event | category | flops | bytes accessed | tf_op | source)
XLA Modules:
  0.0 467.2 jit_solution(8253879368022231031)
XLA Ops:
  7.2 0.8 constant_dynamic-slice_fusion.5
  8.0 0.7 constant_dynamic-slice_fusion.4
  8.7 5.1 %fusion.1 = f32[2048,256]{1,0:T(8,128)} fusion(bf16[1024,256]{1,0:T(8,128)(2,1)} %param.9, bf16[2048,1024]{1,0:T(8,128)(2,1)} %param.8, s32[1024]{0:T(1024)S(1)} %bitcast.137, s32[2048]{0:T(1024)S(1)} %bitcast.135), kind=kOutput, calls=%fused_computation.10 | convolution fusion | flops 1077936128 | bytes 6828032 | tf_op jit(solution)/shard_map/dot_general | solution.py:65
  13.9 4.7 %fusion.54 = f32[2048,256]{1,0:T(8,128)} fusion(bf16[2048,1024]{1,0:T(8,128)(2,1)} %param.8, bf16[1024,256]{1,0:T(8,128)(2,1)S(1)} %copy-done.1), kind=kOutput, calls=%fused_computation.138 | convolution fusion | flops 1073741824 | bytes 6815744 | tf_op jit(solution)/shard_map/dot_general | solution.py:64
  18.8 4.9 %fusion = f32[1024,256]{1,0:T(8,128)} fusion(bf16[2048,256]{1,0:T(8,128)(2,1)S(1)} %copy-done, bf16[2048,1024]{1,0:T(8,128)(2,1)} %param.8, s32[1024]{0:T(1024)S(1)} %bitcast.138, s32[2048]{0:T(1024)S(1)} %bitcast.136), kind=kOutput, calls=%fused_computation.9 | convolution fusion | flops 1077936128 | bytes 6303744 | tf_op jit(solution)/shard_map/dot_general | solution.py:69
  23.7 4.5 fusion.55
  28.2 0.7 fusion.41
  29.6 61.5 %reduce-scatter.7.cloned.1.call-done = f32[128,256]{1,0:T(8,128)} async-done(((f32[2048,256]{1,0:T(8,128)}), f32[128,256]{1,0:T(8,128)}) %reduce-scatter.7.cloned.1.call-update) | async-done | bytes 131088 | tf_op jit(solution)/shard_map/reduce_scatter | solution.py:74
  91.1 77.8 %reduce-scatter.5.cloned.1.call-done = f32[128,256]{1,0:T(8,128)} async-done(((f32[2048,256]{1,0:T(8,128)}), f32[128,256]{1,0:T(8,128)}) %reduce-scatter.5.cloned.1.call-update) | async-done | bytes 131088 | tf_op jit(solution)/shard_map/reduce_scatter | solution.py:73
  168.9 1.5 scatter_custom_fusion
  170.4 0.7 all_to_all.12
  171.1 9.1 %all-to-all-start = ((bf16[128,2,256]{2,1,0:T(2,128)(2,1)}), bf16[128,2,256]{2,1,0:T(2,128)(2,1)S(1)}, u32[]{:S(2)}, u32[]{:S(2)}) async-start(bf16[128,2,256]{2,1,0:T(2,128)(2,1)} %all_to_all.12), calls=%async_computation.2 | async-start | bytes 262144 | tf_op jit(solution)/shard_map/all_to_all | solution.py:97
  180.3 22.3 %reduce-scatter.11.cloned.1.call-done = f32[128,256]{1,0:T(8,128)} async-done(((f32[1024,256]{1,0:T(8,128)}), f32[128,256]{1,0:T(8,128)}) %reduce-scatter.11.cloned.1.call-update) | async-done | bytes 131088 | tf_op jit(solution)/shard_map/reduce_scatter | solution.py:78
  202.6 33.2 %reduce-scatter.9.cloned.1.call-done = f32[128,256]{1,0:T(8,128)} async-done(((f32[1024,256]{1,0:T(8,128)}), f32[128,256]{1,0:T(8,128)}) %reduce-scatter.9.cloned.1.call-update) | async-done | bytes 131088 | tf_op jit(solution)/shard_map/reduce_scatter | solution.py:77
  235.8 1.5 scatter_custom_fusion.1
  237.3 0.7 all_to_all.14
  238.1 10.1 %all-to-all-start.1 = ((bf16[128,2,256]{2,1,0:T(2,128)(2,1)}), bf16[128,2,256]{2,1,0:T(2,128)(2,1)S(1)}, u32[]{:S(2)}, u32[]{:S(2)}) async-start(bf16[128,2,256]{2,1,0:T(2,128)(2,1)} %all_to_all.14), calls=%async_computation.5 | async-start | bytes 262144 | tf_op jit(solution)/shard_map/all_to_all | solution.py:98
  248.1 0.9 multiply_reduce_fusion.4
  250.1 11.7 %cholesky.172 = f32[128,128]{1,0:T(8,128)S(1)} custom-call(f32[128,128]{1,0:T(8,128)S(1)} %cholesky.270), custom_call_target="Cholesky" | custom-call | tf_op jit(solution)/shard_map/jit(cholesky)/cholesky | solution.py:22
  261.9 9.8 %custom-call.15 = f32[1,128,128]{1,2,0:T(8,128)S(1)} custom-call(f32[1,128,128]{2,1,0:T(8,128)S(1)} %get-tuple-element.75), custom_call_target="InvertDiagBlocksLowerTriangular" | custom-call | tf_op jit(solution)/shard_map/jit(cholesky)/cholesky | solution.py:22
  272.2 11.7 %cholesky.189 = f32[128,128]{1,0:T(8,128)S(1)} custom-call(f32[128,128]{1,0:T(8,128)S(1)} %convolution_subtract_fusion.1), custom_call_target="Cholesky" | custom-call | tf_op jit(solution)/shard_map/jit(cholesky)/cholesky | solution.py:22
  283.9 0.7 compare_reduce_fusion.4
  285.9 3.9 while.6
  286.6 1.4 bitcast_dynamic-update-slice_fusion.6
  288.5 1.4 bitcast_dynamic-update-slice_fusion.6
  289.9 19.7 %custom-call.16 = f32[2,128,128]{1,2,0:T(8,128)S(1)} custom-call(f32[2,128,128]{2,1,0:T(8,128)S(1)} %get-tuple-element.24), custom_call_target="InvertDiagBlocksLowerTriangular" | custom-call | tf_op jit(solution)/shard_map/triangular_solve/custom-call.0 | solution.py:23
  310.7 1.3 multiply_reduce_fusion.3
  312.1 1.9 collective-permute-start
  313.9 0.6 fusion.49
  314.5 4.9 %collective-permute-done = f32[256,256]{1,0:T(8,128)S(1)} collective-permute-done((f32[256,256]{1,0:T(8,128)S(1)}, f32[256,256]{1,0:T(8,128)S(1)}, u32[]{:S(2)}, u32[]{:S(2)}) %collective-permute-start) | collective-permute-done | bytes 262176 | tf_op jit(solution)/shard_map/ppermute | solution.py:12
  319.4 0.7 multiply_reduce_fusion.2
  321.3 0.6 fusion.3
  322.1 11.7 %cholesky.206 = f32[128,128]{1,0:T(8,128)S(1)} custom-call(f32[128,128]{1,0:T(8,128)S(1)} %cholesky.273), custom_call_target="Cholesky" | custom-call | tf_op jit(solution)/shard_map/jit(cholesky)/cholesky | solution.py:22
  333.9 9.8 %custom-call.17 = f32[1,128,128]{1,2,0:T(8,128)S(1)} custom-call(f32[1,128,128]{2,1,0:T(8,128)S(1)} %get-tuple-element.71), custom_call_target="InvertDiagBlocksLowerTriangular" | custom-call | tf_op jit(solution)/shard_map/jit(cholesky)/cholesky | solution.py:22
  344.1 11.7 %cholesky.223 = f32[128,128]{1,0:T(8,128)S(1)} custom-call(f32[128,128]{1,0:T(8,128)S(1)} %slice_subtract_fusion.5), custom_call_target="Cholesky" | custom-call | tf_op jit(solution)/shard_map/jit(cholesky)/cholesky | solution.py:22
  355.9 0.6 compare_reduce_fusion.2
  356.5 0.6 compare_reduce_fusion.3
  358.4 4.0 while.7
  358.6 0.6 fusion.84
  359.2 1.3 bitcast_dynamic-update-slice_fusion.7
  361.1 1.3 bitcast_dynamic-update-slice_fusion.7
  362.4 19.7 %custom-call.18 = f32[2,128,128]{1,2,0:T(8,128)S(1)} custom-call(f32[2,128,128]{2,1,0:T(8,128)S(1)} %get-tuple-element.25), custom_call_target="InvertDiagBlocksLowerTriangular" | custom-call | tf_op jit(solution)/shard_map/triangular_solve/custom-call.0 | solution.py:23
  382.1 0.6 fusion.48
  382.7 0.6 convolution_add_fusion.2
  384.2 0.7 multiply_reduce_fusion.1
  384.9 3.8 collective-permute-start.1
  388.7 0.6 fusion.47
  389.3 4.8 %collective-permute-done.1 = f32[256,256]{1,0:T(8,128)S(1)} collective-permute-done((f32[256,256]{1,0:T(8,128)S(1)}, f32[256,256]{1,0:T(8,128)S(1)}, u32[]{:S(2)}, u32[]{:S(2)}) %collective-permute-start.1) | collective-permute-done | bytes 262176 | tf_op jit(solution)/shard_map/ppermute | solution.py:12
  394.1 0.7 multiply_reduce_fusion
  396.2 0.6 fusion.2
  397.0 11.7 %cholesky.240 = f32[128,128]{1,0:T(8,128)S(1)} custom-call(f32[128,128]{1,0:T(8,128)S(1)} %cholesky.276), custom_call_target="Cholesky" | custom-call | tf_op jit(solution)/shard_map/jit(cholesky)/cholesky | solution.py:22
  408.8 9.8 %custom-call.19 = f32[1,128,128]{1,2,0:T(8,128)S(1)} custom-call(f32[1,128,128]{2,1,0:T(8,128)S(1)} %get-tuple-element.67), custom_call_target="InvertDiagBlocksLowerTriangular" | custom-call | tf_op jit(solution)/shard_map/jit(cholesky)/cholesky | solution.py:22
  419.1 11.7 %cholesky.257 = f32[128,128]{1,0:T(8,128)S(1)} custom-call(f32[128,128]{1,0:T(8,128)S(1)} %slice_subtract_fusion.4), custom_call_target="Cholesky" | custom-call | tf_op jit(solution)/shard_map/jit(cholesky)/cholesky | solution.py:22
  430.8 0.7 compare_reduce_fusion
  431.6 0.6 compare_reduce_fusion.1
  433.6 4.3 while.8
  433.8 0.6 fusion.85
  434.4 1.4 bitcast_dynamic-update-slice_fusion.8
  435.9 0.6 fusion.85
  436.5 1.4 bitcast_dynamic-update-slice_fusion.8
  437.9 19.7 %custom-call.20 = f32[2,128,128]{1,2,0:T(8,128)S(1)} custom-call(f32[2,128,128]{2,1,0:T(8,128)S(1)} %get-tuple-element.26), custom_call_target="InvertDiagBlocksLowerTriangular" | custom-call | tf_op jit(solution)/shard_map/triangular_solve/custom-call.0 | solution.py:23
  457.6 0.6 fusion.46
  458.2 0.6 convolution_add_fusion
  459.7 0.7 maximum_bitcast_fusion
  (74 shorter events, 8.2 us)
Async XLA Ops:
  7.2 11.6 %copy-start = (bf16[2048,256]{1,0:T(8,128)(2,1)S(1)}, bf16[2048,256]{1,0:T(8,128)(2,1)}, u32[]{:S(2)}) copy-start(bf16[2048,256]{1,0:T(8,128)(2,1)} %param.10) | copy-start | bytes 3145732
  7.2 83.9 %reduce-scatter.7.cloned.1.call-start = ((), (), s32[]{:S(2)}) async-start(), calls=%async_computation.7 | async-start | bytes 2228224 | tf_op jit(solution)/shard_map/reduce_scatter | solution.py:74
  8.7 5.2 %copy-start.1 = (bf16[1024,256]{1,0:T(8,128)(2,1)S(1)}, bf16[1024,256]{1,0:T(8,128)(2,1)}, u32[]{:S(2)}) copy-start(bf16[1024,256]{1,0:T(8,128)(2,1)} %param.9) | copy-start | bytes 1572868
  13.9 155.0 %reduce-scatter.5.cloned.1.call-start = ((), (), s32[]{:S(2)}) async-start(), calls=%async_computation.6 | async-start | bytes 2228224 | tf_op jit(solution)/shard_map/reduce_scatter | solution.py:73
  18.7 183.9 %reduce-scatter.11.cloned.1.call-start = ((), (), s32[]{:S(2)}) async-start(), calls=%async_computation.9 | async-start | bytes 1179648 | tf_op jit(solution)/shard_map/reduce_scatter | solution.py:78
  23.6 5.3 %copy-start.2 = (s32[128]{0:T(128)S(1)}, s32[128]{0:T(128)}, u32[]{:S(2)}) copy-start(s32[128]{0:T(128)} %param.12) | copy-start | bytes 1540
  23.7 212.2 %reduce-scatter.9.cloned.1.call-start = ((), (), s32[]{:S(2)}) async-start(), calls=%async_computation.8 | async-start | bytes 1179648 | tf_op jit(solution)/shard_map/reduce_scatter | solution.py:77
  171.1 66.9 %all-to-all-start = ((bf16[128,2,256]{2,1,0:T(2,128)(2,1)}), bf16[128,2,256]{2,1,0:T(2,128)(2,1)S(1)}, u32[]{:S(2)}, u32[]{:S(2)}) async-start(bf16[128,2,256]{2,1,0:T(2,128)(2,1)} %all_to_all.12), calls=%async_computation.2 | async-start | bytes 262144 | tf_op jit(solution)/shard_map/all_to_all | solution.py:97
  238.1 71.5 %all-to-all-start.1 = ((bf16[128,2,256]{2,1,0:T(2,128)(2,1)}), bf16[128,2,256]{2,1,0:T(2,128)(2,1)S(1)}, u32[]{:S(2)}, u32[]{:S(2)}) async-start(bf16[128,2,256]{2,1,0:T(2,128)(2,1)} %all_to_all.14), calls=%async_computation.5 | async-start | bytes 262144 | tf_op jit(solution)/shard_map/all_to_all | solution.py:98
  312.1 7.3 %collective-permute-start = (f32[256,256]{1,0:T(8,128)S(1)}, f32[256,256]{1,0:T(8,128)S(1)}, u32[]{:S(2)}, u32[]{:S(2)}) collective-permute-start(f32[256,256]{1,0:T(8,128)S(1)} %get-tuple-element.63), channel_id=1, source_target_pairs={{0,1},{1,0},{2,3},{3,2},{4,5},{5,4},{6,7},{7,6},{8,9},{9,8},{10,11... | collective-permute-start | bytes 786440 | tf_op jit(solution)/shard_map/ppermute | solution.py:12
  384.9 9.2 %collective-permute-start.1 = (f32[256,256]{1,0:T(8,128)S(1)}, f32[256,256]{1,0:T(8,128)S(1)}, u32[]{:S(2)}, u32[]{:S(2)}) collective-permute-start(f32[256,256]{1,0:T(8,128)S(1)} %get-tuple-element.60), channel_id=1, source_target_pairs={{0,2},{1,3},{2,0},{3,1},{4,6},{5,7},{6,4},{7,5},{8,10},{9,11},{10,... | collective-permute-start | bytes 786440 | tf_op jit(solution)/shard_map/ppermute | solution.py:12
Sparse Core Ops, SparseCore 0:
  14.0 77.0 reduce-scatter.6
  94.3 74.5 reduce-scatter.4
  171.3 31.2 reduce-scatter.10
  204.8 30.9 reduce-scatter.8
where the time goes:
time: 475 us; the launch traced here: 467 us
  waiting for transfers between devices  205 us (43%)
  other arithmetic  171 us (36%)
  matrix products  28.5 us (6%)
  starting transfers between devices  25 us (5%)
  between operations  21.5 us (5%)
  local copies, waits for them, and re-layouts  15.9 us (3%)
    another operation x20, other arithmetic, whiten_cross(): jnp.linalg.cholesky(gram_sum + ridge * jnp.eye(width, dtype=jnp.float32))  103 us
    reduce_scatter x1, waiting for transfers between devices, per_device(): lax.psum_scatter(forward_full, 'col', scatter_dimension=0, tiled=True)  77.8 us
    reduce_scatter x1, waiting for transfers between devices, per_device(): lax.psum_scatter(forward_diag, 'col', scatter_dimension=0, tiled=True)  61.5 us
    another operation x7, other arithmetic, whiten_cross(): lax.linalg.triangular_solve(factor, cross_sum, left_side=True, lower=True)  59.1 us
    reduce_scatter x1, waiting for transfers between devices, per_device(): lax.psum_scatter(backward_full, 'row', scatter_dimension=0, tiled=True)  33.2 us
    reduce_scatter x1, waiting for transfers between devices, per_device(): lax.psum_scatter(backward_diag, 'row', scatter_dimension=0, tiled=True)  22.3 us
    another operation x22, local copies, waits for them, and re-layouts, whiten_cross(): lax.linalg.triangular_solve(factor, cross_sum, left_side=True, lower=True)  11.8 us
    all_to_all x1, starting transfers between devices, per_device(): lax.all_to_all(backward_send, ('row', 'col'), split_axis=0, concat_axis=0...  10.1 us
  transfers between devices with their start and end apart: 8, of which 6 were waited for; matrix products, arithmetic and copies ran while one was open for 17% of the time, Pallas kernels for 0%

commit v1 on v0

v1 whole, which is shorter than its diff:
```python
import functools

import jax
import jax.numpy as jnp
from jax import lax
from jax.experimental import pallas as pl
from jax.experimental.pallas import tpu as pltpu
from jax.sharding import PartitionSpec as P

eps = 1e-05
F32, BF16 = jnp.float32, jnp.bfloat16
AB = (((1,), (0,)), ((), ()))
ABT = (((1,), (1,)), ((), ()))
ATB = (((0,), (0,)), ((), ()))


def split(value):
    high = value.astype(BF16)
    return high, (value - high.astype(F32)).astype(BF16)


def mm(left, right, dims=AB):
    return lax.dot_general(left, right, dims, preferred_element_type=F32)


def mm3(left, right, dims=AB):
    return mm(left[0], right[0], dims) + (mm(left[0], right[1], dims) + mm(left[1], right[0], dims))


def whiten(gram, squares, cross, out_ref, b_ref, x_ref, g_ref):
    width = gram.shape[0]
    row = lax.broadcasted_iota(jnp.int32, (width, width), 0)
    col = lax.broadcasted_iota(jnp.int32, (width, width), 1)
    below, diag = row > col, row == col

    def half(value):
        return jnp.where(below, value, jnp.where(diag, 0.5 * value, 0.0))

    def factor(value):
        return jnp.where(below, -value, jnp.where(diag, 1.5 - 0.5 * value, 0.0)).astype(BF16)

    ridge = squares / width + eps
    inv_root = lax.rsqrt(ridge)
    unit = gram * (inv_root * inv_root) + diag.astype(F32)
    g_high, g_low = split(unit)
    g_ref[0] = g_high
    g_ref[1] = g_low
    rhs = split(cross * inv_root)
    square = mm(g_high, g_high)
    fourth = jnp.sum(jnp.sum(square * square, axis=1, keepdims=True), axis=0, keepdims=True)
    scale = 0.99 * lax.rsqrt(jnp.sqrt(fourth))
    fourth_scalar = jnp.sum(fourth)
    steps = jnp.int32(3)
    for k in range(1, 8):
        steps = steps + (fourth_scalar > 2.25 ** (4 * k)).astype(jnp.int32)
    extra = (fourth_scalar > 48.0**4).astype(jnp.int32)

    b0 = unit * scale
    t0 = factor(b0)
    b_ref[...] = mm(mm(t0, b0.astype(BF16)).astype(BF16), t0, ABT)
    x_ref[...] = t0.astype(F32) * jnp.sqrt(scale)

    def step(_, carry):
        b = b_ref[...]
        t = factor(b)
        y = mm(t, b.astype(BF16))
        x = mm(t, x_ref[...].astype(BF16))
        b_ref[...] = mm(y.astype(BF16), t, ABT)
        x_ref[...] = x
        return carry

    lax.fori_loop(1, steps, step, 0)

    def error(x):
        y = split(mm3(x, (g_ref[0], g_ref[1])))
        return half(mm3(y, x, ABT) - diag.astype(F32))

    def fix(_, carry):
        x = split(x_ref[...])
        x_ref[...] = x_ref[...] - mm3(split(error(x)), x)
        return carry

    lax.fori_loop(0, extra, fix, 0)
    x = split(x_ref[...])
    z = mm3(x, rhs)
    out_ref[...] = z - mm(error(x).astype(BF16), z.astype(BF16))


def total(value):
    return jnp.sum(jnp.sum(value, axis=1, keepdims=True), axis=0, keepdims=True)


def leaf_kernel(s_ref, u_ref, out_ref, b_ref, x_ref, g_ref):
    s, u = s_ref[...], u_ref[...]
    wide = s.astype(F32)
    whiten(mm(s, s, ATB), total(wide * wide), mm(s, u, ATB), out_ref, b_ref, x_ref, g_ref)


def merge_kernel(p_ref, q_ref, out_ref, b_ref, x_ref, g_ref):
    p, q = p_ref[...], q_ref[...]
    squares = total(p * p + q * q)
    ps, qs = split(p), split(q)
    gram = mm3(ps, ps, ATB) + mm3(qs, qs, ATB)
    cross = mm3(ps, qs, ATB) + mm3(qs, ps, ATB)
    whiten(gram, squares, cross, out_ref, b_ref, x_ref, g_ref)


def dense_call(kernel, left, right):
    width = left.shape[1]
    whole = pl.BlockSpec(memory_space=pltpu.VMEM)
    return pl.pallas_call(
        kernel,
        out_shape=jax.ShapeDtypeStruct((width, width), F32),
        in_specs=[whole, whole],
        out_specs=whole,
        scratch_shapes=[
            pltpu.VMEM((width, width), F32),
            pltpu.VMEM((width, width), F32),
            pltpu.VMEM((2, width, width), BF16),
        ],
    )(left, right)


def from_partner(value, axis, distance):
    mask = 2**distance
    pairs = [(source, source ^ mask) for source in range(lax.axis_size(axis))]
    return lax.ppermute(value, axis, pairs)


def spread(rows, block_leaf, places, capacity, devices):
    count = rows.shape[0]
    positions = jnp.arange(devices, dtype=jnp.int32)
    owner = jnp.sum(jnp.where(block_leaf[:, None] == positions[None, :], places[None, :], 0), axis=1)
    order = jnp.arange(count, dtype=jnp.int32)
    earlier = (owner[:, None] == owner[None, :]) & (order[None, :] < order[:, None])
    slot = owner * capacity + jnp.sum(earlier.astype(jnp.int32), axis=1)
    chosen = (jnp.arange(devices * capacity, dtype=jnp.int32)[:, None] == slot[None, :]).astype(BF16)
    return jnp.dot(chosen, rows, preferred_element_type=F32).astype(BF16)


def per_device(front_block, probe_right, probe_left, row_leaf, tree_leaf):
    row_count = lax.axis_size("row")
    col_count = lax.axis_size("col")
    devices = row_count * col_count
    row_index = lax.axis_index("row")
    col_index = lax.axis_index("col")
    tile_rows, tile_cols = front_block.shape
    samples = probe_right.shape[1]
    leaves = row_leaf[:, 0]
    rows_dev = leaves.shape[0] // devices
    capacity = 2
    rows_leaf = lax.dynamic_slice_in_dim(leaves, row_index * tile_rows, tile_rows)
    cols_leaf = lax.dynamic_slice_in_dim(leaves, col_index * tile_cols, tile_cols)
    same_leaf = rows_leaf[:, None] == cols_leaf[None, :]
    off = jnp.where(same_leaf, jnp.zeros_like(front_block), front_block)
    forward = jnp.dot(off, probe_right, preferred_element_type=F32).astype(BF16)
    backward = lax.dot_general(off, probe_left, ATB, preferred_element_type=F32)
    forward = lax.all_to_all(forward.reshape(col_count, rows_dev, samples), "col", 0, 0, tiled=True)
    backward = lax.all_to_all(backward.reshape(row_count, rows_dev, samples), "row", 0, 0, tiled=True)
    sample_rows = jnp.sum(forward.astype(F32), axis=0).astype(BF16)
    sample_back = jnp.sum(backward, axis=0).astype(BF16)
    positions = jnp.arange(devices, dtype=jnp.int32)
    places = jnp.sum(jnp.where(tree_leaf[:, None] == positions[None, :], positions[:, None], 0), axis=0)

    def block_leaf(block):
        return lax.dynamic_slice_in_dim(leaves, block * rows_dev, rows_dev)

    forward_send = spread(sample_rows, block_leaf(row_index * col_count + col_index), places, capacity, devices)
    backward_send = spread(sample_back, block_leaf(col_index * row_count + row_index), places, capacity, devices)
    both = jnp.stack(
        [forward_send.reshape(devices, capacity, samples), backward_send.reshape(devices, capacity, samples)], axis=1
    )
    both = lax.all_to_all(both, ("row", "col"), split_axis=0, concat_axis=0, tiled=True)
    forward_recv = both[:, 0].reshape(devices * capacity, samples)
    backward_recv = both[:, 1].reshape(row_count, col_count, capacity, samples)
    backward_recv = backward_recv.transpose(1, 0, 2, 3).reshape(devices * capacity, samples)
    coupling = dense_call(leaf_kernel, forward_recv, backward_recv)
    merged = coupling
    for level in range(2):
        merged = dense_call(merge_kernel, merged, from_partner(merged, "col", level))
    return (coupling[None], merged[None])


def solution(mesh):
    return jax.shard_map(
        per_device,
        mesh=mesh,
        in_specs=(P("row", "col"), P("col", None), P("row", None), P(), P()),
        out_specs=(P(("row", "col"), None, None), P(("row", "col"), None, None)),
        check_vma=False,
    )
```

time: 475 us -> 105 us (0.22); the launches traced: 467 us -> 104 us
  other arithmetic: 171 us -> 1.2 us
  waiting for transfers between devices: 205 us -> 38.2 us
  between operations: 21.5 us -> 0.76 us
  matrix products: 28.5 us -> 9.95 us
  blocking collectives: 0 us -> 17.4 us
  Pallas kernels: 0 us -> 16.4 us
  local copies, waits for them, and re-layouts: 15.9 us -> 5.42 us
  starting transfers between devices: 25 us -> 14.8 us
    reduce_scatter x4 -> x0, waiting for transfers between devices: 195 us -> none  [the longest x1 77.8 us: per_device(): lax.psum_scatter(forward_full, 'col', scatter_dimension=0, tiled=True)]
    another operation x27 -> x1, other arithmetic: 162 us -> 0.34 us  [per_device(): jnp.stack([forward_send.reshape(devices, capacity, samples), backward_sen...]
    all_to_all x2, waiting for transfers between devices: 0.01 us -> 24.1 us  [the longest x1 14.6 us: per_device(): lax.all_to_all(forward.reshape(col_count, rows_dev, samples), 'col', 0, 0...]
    all_to_all x0 -> x1, blocking collectives: none -> 17.4 us  [per_device(): lax.all_to_all(both, ('row', 'col'), split_axis=0, concat_axis=0, tiled=T...]
    pallas_call x0 -> x3, Pallas kernels: none -> 16.4 us  [dense_call(): pl.pallas_call(kernel, out_shape=jax.ShapeDtypeStruct((width, width), F32...]
    dot_general x14 -> x4, matrix products: 24.5 us -> 9.95 us  [the longest x1 4.93 us: per_device(): backward = lax.dot_general(off, probe_left, ATB, preferred_element_type=F32)]
    another operation x28 -> x3, local copies, waits for them, and re-layouts: 11.9 us -> 0.83 us  [the longest x1 0.71 us: per_device(): forward_recv = both[:, 0].reshape(devices * capacity, samples)]
    all_to_all x2, starting transfers between devices: 19.2 us -> 13.6 us  [the longest x1 7.77 us: per_device(): lax.all_to_all(forward.reshape(col_count, rows_dev, samples), 'col', 0, 0...]
  transfers between devices with their start and end apart: 8 -> 4, of which waited for: 6 -> 4; matrix products, arithmetic and copies ran while one was open for 17% -> 6% of each run, Pallas kernels for 0% -> 0%
where the time goes in v1:
time: 105 us; the launch traced here: 104 us
  waiting for transfers between devices  38.2 us (36%)
  blocking collectives  17.4 us (17%)
  Pallas kernels  16.4 us (16%)
  starting transfers between devices  14.8 us (14%)
  matrix products  9.95 us (9%)
  local copies, waits for them, and re-layouts  5.42 us (5%)
  other arithmetic  1.2 us (1%)
    all_to_all x1, blocking collectives, per_device(): lax.all_to_all(both, ('row', 'col'), split_axis=0, concat_axis=0, tiled=T...  17.4 us
    pallas_call x3, Pallas kernels, dense_call(): pl.pallas_call(kernel, out_shape=jax.ShapeDtypeStruct((width, width), F32...  16.4 us
    all_to_all x1, waiting for transfers between devices, per_device(): lax.all_to_all(forward.reshape(col_count, rows_dev, samples), 'col', 0, 0...  14.6 us
    ppermute x2, waiting for transfers between devices, from_partner(): return lax.ppermute(value, axis, pairs)  14.2 us
    all_to_all x1, waiting for transfers between devices, per_device(): lax.all_to_all(backward.reshape(row_count, rows_dev, samples), 'row', 0,...  9.5 us
    all_to_all x1, starting transfers between devices, per_device(): lax.all_to_all(forward.reshape(col_count, rows_dev, samples), 'col', 0, 0...  7.77 us
    all_to_all x1, starting transfers between devices, per_device(): lax.all_to_all(backward.reshape(row_count, rows_dev, samples), 'row', 0,...  5.79 us
    dot_general x1, matrix products, per_device(): backward = lax.dot_general(off, probe_left, ATB, preferred_element_type=F32)  4.93 us
  transfers between devices with their start and end apart: 4, of which 4 were waited for; matrix products, arithmetic and copies ran while one was open for 6% of the time, Pallas kernels for 0%

profile of v1, /device:TPU:1, one launch (start us, length us, event | category | flops | bytes accessed | tf_op | source)
XLA Modules:
  0.0 104.1 jit_solution(11663683581513948412)
XLA Ops:
  0.6 0.0 copy-start
  0.7 0.8 constant_dynamic-slice_fusion.1
  1.4 0.7 constant_dynamic-slice_fusion.2
  2.1 0.0 copy-done
  2.1 0.0 copy-start.4
  2.1 0.0 copy-start.3
  2.1 4.9 %fusion = f32[1024,256]{1,0:T(8,128)} fusion(bf16[2048,256]{1,0:T(8,128)(2,1)S(1)} %copy-done, bf16[2048,1024]{1,0:T(8,128)(2,1)} %param.5, s32[1024]{0:T(1024)S(1)} %bitcast.27, s32[2048]{0:T(1024)S(1)} %bitcast.25), kind=kOutput, calls=%fused_computation.2 | convolution fusion | flops 1077936128 | bytes 6303744 | tf_op jit(solution)/shard_map/dot_general | solution.py:157
  7.1 5.8 %all-to-all-start.1 = ((f32[8,128,256]{2,1,0:T(8,128)}), f32[8,128,256]{2,1,0:T(8,128)S(1)}, u32[]{:S(2)}, u32[]{:S(2)}) async-start(f32[8,128,256]{2,1,0:T(8,128)} %bitcast.6), calls=%async_computation.1 | async-start | bytes 2097152 | tf_op jit(solution)/shard_map/all_to_all | solution.py:159
  12.9 0.7 fusion.7
  13.5 0.0 copy-done.4
  13.5 0.1 select_reduce_fusion.2
  13.6 0.0 copy-done.3
  13.6 4.7 %convolution_convert_fusion = bf16[2048,256]{1,0:T(8,128)(2,1)} fusion(bf16[1024,256]{1,0:T(8,128)(2,1)S(1)} %copy-done.3, bf16[2048,1024]{1,0:T(8,128)(2,1)} %param.5, s32[1024]{0:T(1024)S(1)} %bitcast.28, s32[2048]{0:T(1024)S(1)} %bitcast.26), kind=kOutput, calls=%fused_computation.1 | convolution fusion | flops 1078460416 | bytes 5779456 | tf_op jit(solution)/shard_map/dot_general | solution.py:156
  18.3 9.5 %all-to-all-done.1 = f32[8,128,256]{2,1,0:T(8,128)S(1)} async-done(((f32[8,128,256]{2,1,0:T(8,128)}), f32[8,128,256]{2,1,0:T(8,128)S(1)}, u32[]{:S(2)}, u32[]{:S(2)}) %all-to-all-start.1) | async-done | bytes 1048608 | tf_op jit(solution)/shard_map/all_to_all | solution.py:159
  27.8 7.8 %all-to-all-start = ((bf16[16,128,256]{2,1,0:T(8,128)(2,1)}), bf16[16,128,256]{2,1,0:T(8,128)(2,1)S(1)}, u32[]{:S(2)}, u32[]{:S(2)}) async-start(bf16[16,128,256]{2,1,0:T(8,128)(2,1)} %bitcast.20), calls=%async_computation | async-start | bytes 2097152 | tf_op jit(solution)/shard_map/all_to_all | solution.py:158
  35.6 0.2 select_reduce_fusion.1
  35.8 0.2 convert_reduce_fusion.1
  36.0 0.2 convert_reduce_fusion
  36.2 0.1 reduce_sum.72
  36.2 0.2 convolution_convert_fusion.1
  36.4 0.1 stack_reshape.7
  36.5 14.6 %all-to-all-done = bf16[16,128,256]{2,1,0:T(8,128)(2,1)S(1)} async-done(((bf16[16,128,256]{2,1,0:T(8,128)(2,1)}), bf16[16,128,256]{2,1,0:T(8,128)(2,1)S(1)}, u32[]{:S(2)}, u32[]{:S(2)}) %all-to-all-start) | async-done | bytes 1048608 | tf_op jit(solution)/shard_map/all_to_all | solution.py:158
  51.1 0.1 reduce_sum.69
  51.2 0.2 convolution_convert_fusion.2
  51.4 0.1 stack_reshape.6
  51.5 0.3 pad_maximum_fusion
  51.8 17.4 %all_to_all.15 = bf16[128,2,2,256]{3,2,1,0:T(2,128)(2,1)S(1)} all-to-all(bf16[128,2,2,256]{3,2,1,0:T(2,128)(2,1)S(1)} %pad_maximum_fusion), channel_id=1, replica_groups=mesh['row'=8,'col'=16] {'row','col'}, dimensions={0} | all-to-all | bytes 524288 | tf_op jit(solution)/shard_map/all_to_all | solution.py:173
  69.2 0.2 fusion.10
  69.4 0.1 copy.18
  69.5 0.7 reshape.42.u_ref
  70.2 0.7 reshape_squeeze.6.s_ref
  70.9 5.4 %shard_map.68.p_ref = f32[256,256]{1,0:T(8,128)} custom-call(bf16[256,256]{1,0:T(8,128)(2,1)} %reshape_squeeze.6.s_ref, bf16[256,256]{1,0:T(8,128)(2,1)} %reshape.42.u_ref), custom_call_target="tpu_custom_call" | custom-call | tf_op jit(solution)/shard_map/pallas_call | solution.py:111
  76.4 0.6 collective-permute-start
  76.9 6.8 %collective-permute-done.q_ref = f32[256,256]{1,0:T(8,128)S(1)} collective-permute-done((f32[256,256]{1,0:T(8,128)}, f32[256,256]{1,0:T(8,128)S(1)}, u32[]{:S(2)}, u32[]{:S(2)}) %collective-permute-start) | collective-permute-done | bytes 262176 | tf_op jit(solution)/shard_map/ppermute | solution.py:127
  83.7 0.0 copy-start.2
  83.7 0.7 copy-done.2
  84.4 5.5 %shard_map.69.p_ref = f32[256,256]{1,0:T(8,128)} custom-call(f32[256,256]{1,0:T(8,128)} %shard_map.68.p_ref, f32[256,256]{1,0:T(8,128)} %copy-done.2), custom_call_target="tpu_custom_call" | custom-call | tf_op jit(solution)/shard_map/pallas_call | solution.py:111
  89.9 0.7 collective-permute-start.1
  90.6 7.3 %collective-permute-done.1.q_ref = f32[256,256]{1,0:T(8,128)S(1)} collective-permute-done((f32[256,256]{1,0:T(8,128)}, f32[256,256]{1,0:T(8,128)S(1)}, u32[]{:S(2)}, u32[]{:S(2)}) %collective-permute-start.1) | collective-permute-done | bytes 262176 | tf_op jit(solution)/shard_map/ppermute | solution.py:127
  97.9 0.0 copy-start.1
  97.9 0.7 copy-done.1
  98.6 5.5 %shard_map.70 = f32[256,256]{1,0:T(8,128)} custom-call(f32[256,256]{1,0:T(8,128)} %shard_map.69.p_ref, f32[256,256]{1,0:T(8,128)} %copy-done.1), custom_call_target="tpu_custom_call" | custom-call | tf_op jit(solution)/shard_map/pallas_call | solution.py:111
  (3 shorter events, 0.0 us)
Async XLA Ops:
  0.6 1.5 %copy-start = (bf16[2048,256]{1,0:T(8,128)(2,1)S(1)}, bf16[2048,256]{1,0:T(8,128)(2,1)}, u32[]{:S(2)}) copy-start(bf16[2048,256]{1,0:T(8,128)(2,1)} %param.7) | copy-start | bytes 3145732
  2.1 11.4 %copy-start.4 = (s32[128]{0:T(128)S(1)}, s32[128]{0:T(128)}, u32[]{:S(2)}) copy-start(s32[128]{0:T(128)} %param.9) | copy-start | bytes 1540
  2.1 11.5 %copy-start.3 = (bf16[1024,256]{1,0:T(8,128)(2,1)S(1)}, bf16[1024,256]{1,0:T(8,128)(2,1)}, u32[]{:S(2)}) copy-start(bf16[1024,256]{1,0:T(8,128)(2,1)} %param.6) | copy-start | bytes 1572868
  7.1 20.8 %all-to-all-start.1 = ((f32[8,128,256]{2,1,0:T(8,128)}), f32[8,128,256]{2,1,0:T(8,128)S(1)}, u32[]{:S(2)}, u32[]{:S(2)}) async-start(f32[8,128,256]{2,1,0:T(8,128)} %bitcast.6), calls=%async_computation.1 | async-start | bytes 2097152 | tf_op jit(solution)/shard_map/all_to_all | solution.py:159
  27.8 23.3 %all-to-all-start = ((bf16[16,128,256]{2,1,0:T(8,128)(2,1)}), bf16[16,128,256]{2,1,0:T(8,128)(2,1)S(1)}, u32[]{:S(2)}, u32[]{:S(2)}) async-start(bf16[16,128,256]{2,1,0:T(8,128)(2,1)} %bitcast.20), calls=%async_computation | async-start | bytes 2097152 | tf_op jit(solution)/shard_map/all_to_all | solution.py:158
  76.4 7.4 %collective-permute-start = (f32[256,256]{1,0:T(8,128)}, f32[256,256]{1,0:T(8,128)S(1)}, u32[]{:S(2)}, u32[]{:S(2)}) collective-permute-start(f32[256,256]{1,0:T(8,128)} %shard_map.68.p_ref), channel_id=1, source_target_pairs={{0,1},{1,0},{2,3},{3,2},{4,5},{5,4},{6,7},{7,6},{8,9},{9,8},{10,11... | collective-permute-start | bytes 786440 | tf_op jit(solution)/shard_map/ppermute | solution.py:127
  83.7 0.7 copy-start.2
  89.9 8.0 %collective-permute-start.1 = (f32[256,256]{1,0:T(8,128)}, f32[256,256]{1,0:T(8,128)S(1)}, u32[]{:S(2)}, u32[]{:S(2)}) collective-permute-start(f32[256,256]{1,0:T(8,128)} %shard_map.69.p_ref), channel_id=1, source_target_pairs={{0,2},{1,3},{2,0},{3,1},{4,6},{5,7},{6,4},{7,5},{8,10},{9,11},{10,... | collective-permute-start | bytes 786440 | tf_op jit(solution)/shard_map/ppermute | solution.py:127
  97.9 0.7 copy-start.1

commit v2 on v1

--- a/solution.py
+++ b/solution.py
@@ -27,7 +27,7 @@
     return mm(left[0], right[0], dims) + (mm(left[0], right[1], dims) + mm(left[1], right[0], dims))
 
 
-def whiten(gram, squares, cross, out_ref, b_ref, x_ref, g_ref):
+def whiten(gram, squares, cross, out_ref, send_ref, b_ref, x_ref, g_ref):
     width = gram.shape[0]
     row = lax.broadcasted_iota(jnp.int32, (width, width), 0)
     col = lax.broadcasted_iota(jnp.int32, (width, width), 1)
@@ -83,26 +83,29 @@
     lax.fori_loop(0, extra, fix, 0)
     x = split(x_ref[...])
     z = mm3(x, rhs)
-    out_ref[...] = z - mm(error(x).astype(BF16), z.astype(BF16))
+    out = z - mm(error(x).astype(BF16), z.astype(BF16))
+    out_ref[...] = out
+    send_ref[...] = out.astype(BF16)
 
 
 def total(value):
     return jnp.sum(jnp.sum(value, axis=1, keepdims=True), axis=0, keepdims=True)
 
 
-def leaf_kernel(s_ref, u_ref, out_ref, b_ref, x_ref, g_ref):
+def leaf_kernel(s_ref, u_ref, out_ref, *refs):
     s, u = s_ref[...], u_ref[...]
     wide = s.astype(F32)
-    whiten(mm(s, s, ATB), total(wide * wide), mm(s, u, ATB), out_ref, b_ref, x_ref, g_ref)
+    whiten(mm(s, s, ATB), total(wide * wide), mm(s, u, ATB), out_ref, *refs)
 
 
-def merge_kernel(p_ref, q_ref, out_ref, b_ref, x_ref, g_ref):
+def merge_kernel(p_ref, q_ref, out_ref, *refs):
     p, q = p_ref[...], q_ref[...]
-    squares = total(p * p + q * q)
-    ps, qs = split(p), split(q)
-    gram = mm3(ps, ps, ATB) + mm3(qs, qs, ATB)
-    cross = mm3(ps, qs, ATB) + mm3(qs, ps, ATB)
-    whiten(gram, squares, cross, out_ref, b_ref, x_ref, g_ref)
+    wide = q.astype(F32)
+    squares = total(p * p + wide * wide)
+    high, low = split(p)
+    gram = mm3((high, low), (high, low), ATB) + mm(q, q, ATB)
+    cross = mm(high, q, ATB) + mm(low, q, ATB)
+    whiten(gram, squares, cross + cross.T, out_ref, *refs)
 
 
 def dense_call(kernel, left, right):
@@ -110,9 +113,9 @@
     whole = pl.BlockSpec(memory_space=pltpu.VMEM)
     return pl.pallas_call(
         kernel,
-        out_shape=jax.ShapeDtypeStruct((width, width), F32),
+        out_shape=(jax.ShapeDtypeStruct((width, width), F32), jax.ShapeDtypeStruct((width, width), BF16)),
         in_specs=[whole, whole],
-        out_specs=whole,
+        out_specs=(whole, whole),
         scratch_shapes=[
             pltpu.VMEM((width, width), F32),
             pltpu.VMEM((width, width), F32),
@@ -174,10 +177,10 @@
     forward_recv = both[:, 0].reshape(devices * capacity, samples)
     backward_recv = both[:, 1].reshape(row_count, col_count, capacity, samples)
     backward_recv = backward_recv.transpose(1, 0, 2, 3).reshape(devices * capacity, samples)
-    coupling = dense_call(leaf_kernel, forward_recv, backward_recv)
+    coupling, sent = dense_call(leaf_kernel, forward_recv, backward_recv)
     merged = coupling
     for level in range(2):
-        merged = dense_call(merge_kernel, merged, from_partner(merged, "col", level))
+        merged, sent = dense_call(merge_kernel, merged, from_partner(sent, "col", level))
     return (coupling[None], merged[None])
 
 

time: 105 us -> 100 us (0.952)
  waiting for transfers between devices: 38.2 us -> 32.3 us
    ppermute x2, waiting for transfers between devices: 14.2 us -> 8.2 us  [from_partner(): return lax.ppermute(value, axis, pairs)]
where the time goes in v2:
time: 100 us; the launch traced here: 98.1 us
  waiting for transfers between devices  32.3 us (32%)
  blocking collectives  17.4 us (17%)
  Pallas kernels  15.8 us (16%)
  starting transfers between devices  15.4 us (15%)
  matrix products  9.95 us (10%)
  local copies, waits for them, and re-layouts  5.33 us (5%)
  other arithmetic  1.2 us (1%)
    all_to_all x1, blocking collectives, per_device(): lax.all_to_all(both, ('row', 'col'), split_axis=0, concat_axis=0, tiled=T...  17.4 us
    pallas_call x3, Pallas kernels, dense_call(): pl.pallas_call(kernel, out_shape=(jax.ShapeDtypeStruct((width, width), F3...  15.8 us
    all_to_all x1, waiting for transfers between devices, per_device(): lax.all_to_all(forward.reshape(col_count, rows_dev, samples), 'col', 0, 0...  14.6 us
    all_to_all x1, waiting for transfers between devices, per_device(): lax.all_to_all(backward.reshape(row_count, rows_dev, samples), 'row', 0,...  9.5 us
    ppermute x2, waiting for transfers between devices, from_partner(): return lax.ppermute(value, axis, pairs)  8.2 us
    all_to_all x1, starting transfers between devices, per_device(): lax.all_to_all(forward.reshape(col_count, rows_dev, samples), 'col', 0, 0...  7.77 us
    all_to_all x1, starting transfers between devices, per_device(): lax.all_to_all(backward.reshape(row_count, rows_dev, samples), 'row', 0,...  5.79 us
    dot_general x1, matrix products, per_device(): backward = lax.dot_general(off, probe_left, ATB, preferred_element_type=F32)  4.93 us
  transfers between devices with their start and end apart: 4, of which 4 were waited for; matrix products, arithmetic and copies ran while one was open for 6% of the time, Pallas kernels for 0%

profile of v2, /device:TPU:1, one launch (start us, length us, event | category | flops | bytes accessed | tf_op | source)
XLA Modules:
  0.0 98.1 jit_solution(17108149378638361071)
XLA Ops:
  0.6 0.0 copy-start
  0.7 0.8 constant_dynamic-slice_fusion.1
  1.4 0.7 constant_dynamic-slice_fusion.2
  2.1 0.0 copy-done
  2.1 0.0 copy-start.4
  2.1 0.0 copy-start.3
  2.1 4.9 %fusion = f32[1024,256]{1,0:T(8,128)} fusion(bf16[2048,256]{1,0:T(8,128)(2,1)S(1)} %copy-done, bf16[2048,1024]{1,0:T(8,128)(2,1)} %param.5, s32[1024]{0:T(1024)S(1)} %bitcast.26, s32[2048]{0:T(1024)S(1)} %bitcast.24), kind=kOutput, calls=%fused_computation.2 | convolution fusion | flops 1077936128 | bytes 6303744 | tf_op jit(solution)/shard_map/dot_general | solution.py:160
  7.1 5.8 %all-to-all-start.1 = ((f32[8,128,256]{2,1,0:T(8,128)}), f32[8,128,256]{2,1,0:T(8,128)S(1)}, u32[]{:S(2)}, u32[]{:S(2)}) async-start(f32[8,128,256]{2,1,0:T(8,128)} %bitcast.6), calls=%async_computation.1 | async-start | bytes 2097152 | tf_op jit(solution)/shard_map/all_to_all | solution.py:162
  12.9 0.7 fusion.7
  13.5 0.0 copy-done.4
  13.5 0.1 select_reduce_fusion.2
  13.6 0.0 copy-done.3
  13.6 4.7 %convolution_convert_fusion = bf16[2048,256]{1,0:T(8,128)(2,1)} fusion(bf16[1024,256]{1,0:T(8,128)(2,1)S(1)} %copy-done.3, bf16[2048,1024]{1,0:T(8,128)(2,1)} %param.5, s32[1024]{0:T(1024)S(1)} %bitcast.27, s32[2048]{0:T(1024)S(1)} %bitcast.25), kind=kOutput, calls=%fused_computation.1 | convolution fusion | flops 1078460416 | bytes 5779456 | tf_op jit(solution)/shard_map/dot_general | solution.py:159
  18.3 9.5 %all-to-all-done.1 = f32[8,128,256]{2,1,0:T(8,128)S(1)} async-done(((f32[8,128,256]{2,1,0:T(8,128)}), f32[8,128,256]{2,1,0:T(8,128)S(1)}, u32[]{:S(2)}, u32[]{:S(2)}) %all-to-all-start.1) | async-done | bytes 1048608 | tf_op jit(solution)/shard_map/all_to_all | solution.py:162
  27.8 7.8 %all-to-all-start = ((bf16[16,128,256]{2,1,0:T(8,128)(2,1)}), bf16[16,128,256]{2,1,0:T(8,128)(2,1)S(1)}, u32[]{:S(2)}, u32[]{:S(2)}) async-start(bf16[16,128,256]{2,1,0:T(8,128)(2,1)} %bitcast.19), calls=%async_computation | async-start | bytes 2097152 | tf_op jit(solution)/shard_map/all_to_all | solution.py:161
  35.6 0.2 select_reduce_fusion.1
  35.8 0.2 convert_reduce_fusion.1
  36.0 0.2 convert_reduce_fusion
  36.2 0.1 reduce_sum.72
  36.2 0.2 convolution_convert_fusion.1
  36.4 0.1 stack_reshape.7
  36.5 14.6 %all-to-all-done = bf16[16,128,256]{2,1,0:T(8,128)(2,1)S(1)} async-done(((bf16[16,128,256]{2,1,0:T(8,128)(2,1)}), bf16[16,128,256]{2,1,0:T(8,128)(2,1)S(1)}, u32[]{:S(2)}, u32[]{:S(2)}) %all-to-all-start) | async-done | bytes 1048608 | tf_op jit(solution)/shard_map/all_to_all | solution.py:161
  51.1 0.1 reduce_sum.69
  51.2 0.2 convolution_convert_fusion.2
  51.4 0.1 stack_reshape.6
  51.5 0.3 pad_maximum_fusion
  51.8 17.4 %all_to_all.15 = bf16[128,2,2,256]{3,2,1,0:T(2,128)(2,1)S(1)} all-to-all(bf16[128,2,2,256]{3,2,1,0:T(2,128)(2,1)S(1)} %pad_maximum_fusion), channel_id=1, replica_groups=mesh['row'=8,'col'=16] {'row','col'}, dimensions={0} | all-to-all | bytes 524288 | tf_op jit(solution)/shard_map/all_to_all | solution.py:176
  69.2 0.2 fusion.10
  69.4 0.1 copy.18
  69.5 0.7 reshape.42.u_ref
  70.2 0.7 reshape_squeeze.6.s_ref
  70.9 5.1 %shard_map.68 = (f32[256,256]{1,0:T(8,128)}, bf16[256,256]{1,0:T(8,128)(2,1)}) custom-call(bf16[256,256]{1,0:T(8,128)(2,1)} %reshape_squeeze.6.s_ref, bf16[256,256]{1,0:T(8,128)(2,1)} %reshape.42.u_ref), custom_call_target="tpu_custom_call" | custom-call | tf_op jit(solution)/shard_map/pallas_call | solution.py:114
  76.1 0.5 collective-permute-start
  76.6 4.0 %collective-permute-done.q_ref = bf16[256,256]{1,0:T(8,128)(2,1)S(1)} collective-permute-done((bf16[256,256]{1,0:T(8,128)(2,1)}, bf16[256,256]{1,0:T(8,128)(2,1)S(1)}, u32[]{:S(2)}, u32[]{:S(2)}) %collective-permute-start) | collective-permute-done | bytes 131104 | tf_op jit(solution)/shard_map/ppermute | solution.py:130
  80.6 0.0 copy-start.2
  80.6 0.7 copy-done.2
  81.3 5.3 %shard_map.69 = (f32[256,256]{1,0:T(8,128)}, bf16[256,256]{1,0:T(8,128)(2,1)}) custom-call(f32[256,256]{1,0:T(8,128)} %get-tuple-element.7.p_ref, bf16[256,256]{1,0:T(8,128)(2,1)} %copy-done.2), custom_call_target="tpu_custom_call" | custom-call | tf_op jit(solution)/shard_map/pallas_call | solution.py:114
  86.6 1.3 %collective-permute-start.1 = (bf16[256,256]{1,0:T(8,128)(2,1)}, bf16[256,256]{1,0:T(8,128)(2,1)S(1)}, u32[]{:S(2)}, u32[]{:S(2)}) collective-permute-start(bf16[256,256]{1,0:T(8,128)(2,1)} %get-tuple-element.10), channel_id=1, source_target_pairs={{0,2},{1,3},{2,0},{3,1},{4,6},{5,7},{6,4},{7,5},{8,10},{9,11},{10,... | collective-permute-start | bytes 393224 | tf_op jit(solution)/shard_map/ppermute | solution.py:130
  88.0 4.2 %collective-permute-done.1.q_ref = bf16[256,256]{1,0:T(8,128)(2,1)S(1)} collective-permute-done((bf16[256,256]{1,0:T(8,128)(2,1)}, bf16[256,256]{1,0:T(8,128)(2,1)S(1)}, u32[]{:S(2)}, u32[]{:S(2)}) %collective-permute-start.1) | collective-permute-done | bytes 131104 | tf_op jit(solution)/shard_map/ppermute | solution.py:130
  92.2 0.0 copy-start.1
  92.2 0.7 copy-done.1
  92.8 5.3 %shard_map.70 = (f32[256,256]{1,0:T(8,128)}, bf16[256,256]{1,0:T(8,128)(2,1)}) custom-call(f32[256,256]{1,0:T(8,128)} %get-tuple-element.9.p_ref, bf16[256,256]{1,0:T(8,128)(2,1)} %copy-done.1), custom_call_target="tpu_custom_call" | custom-call | tf_op jit(solution)/shard_map/pallas_call | solution.py:114
  (3 shorter events, 0.0 us)
Async XLA Ops:
  0.6 1.5 %copy-start = (bf16[2048,256]{1,0:T(8,128)(2,1)S(1)}, bf16[2048,256]{1,0:T(8,128)(2,1)}, u32[]{:S(2)}) copy-start(bf16[2048,256]{1,0:T(8,128)(2,1)} %param.7) | copy-start | bytes 3145732
  2.1 11.4 %copy-start.4 = (s32[128]{0:T(128)S(1)}, s32[128]{0:T(128)}, u32[]{:S(2)}) copy-start(s32[128]{0:T(128)} %param.9) | copy-start | bytes 1540
  2.1 11.5 %copy-start.3 = (bf16[1024,256]{1,0:T(8,128)(2,1)S(1)}, bf16[1024,256]{1,0:T(8,128)(2,1)}, u32[]{:S(2)}) copy-start(bf16[1024,256]{1,0:T(8,128)(2,1)} %param.6) | copy-start | bytes 1572868
  7.1 20.8 %all-to-all-start.1 = ((f32[8,128,256]{2,1,0:T(8,128)}), f32[8,128,256]{2,1,0:T(8,128)S(1)}, u32[]{:S(2)}, u32[]{:S(2)}) async-start(f32[8,128,256]{2,1,0:T(8,128)} %bitcast.6), calls=%async_computation.1 | async-start | bytes 2097152 | tf_op jit(solution)/shard_map/all_to_all | solution.py:162
  27.8 23.3 %all-to-all-start = ((bf16[16,128,256]{2,1,0:T(8,128)(2,1)}), bf16[16,128,256]{2,1,0:T(8,128)(2,1)S(1)}, u32[]{:S(2)}, u32[]{:S(2)}) async-start(bf16[16,128,256]{2,1,0:T(8,128)(2,1)} %bitcast.19), calls=%async_computation | async-start | bytes 2097152 | tf_op jit(solution)/shard_map/all_to_all | solution.py:161
  76.1 4.6 %collective-permute-start = (bf16[256,256]{1,0:T(8,128)(2,1)}, bf16[256,256]{1,0:T(8,128)(2,1)S(1)}, u32[]{:S(2)}, u32[]{:S(2)}) collective-permute-start(bf16[256,256]{1,0:T(8,128)(2,1)} %get-tuple-element.8), channel_id=1, source_target_pairs={{0,1},{1,0},{2,3},{3,2},{4,5},{5,4},{6,7},{7,6},{8,9},{9,8},{10,11... | collective-permute-start | bytes 393224 | tf_op jit(solution)/shard_map/ppermute | solution.py:130
  80.6 0.7 copy-start.2
  86.6 5.5 %collective-permute-start.1 = (bf16[256,256]{1,0:T(8,128)(2,1)}, bf16[256,256]{1,0:T(8,128)(2,1)S(1)}, u32[]{:S(2)}, u32[]{:S(2)}) collective-permute-start(bf16[256,256]{1,0:T(8,128)(2,1)} %get-tuple-element.10), channel_id=1, source_target_pairs={{0,2},{1,3},{2,0},{3,1},{4,6},{5,7},{6,4},{7,5},{8,10},{9,11},{10,... | collective-permute-start | bytes 393224 | tf_op jit(solution)/shard_map/ppermute | solution.py:130
  92.2 0.7 copy-start.1

commit v3 on v2

--- a/solution.py
+++ b/solution.py
@@ -130,53 +130,274 @@
     return lax.ppermute(value, axis, pairs)
 
 
-def spread(rows, block_leaf, places, capacity, devices):
-    count = rows.shape[0]
-    positions = jnp.arange(devices, dtype=jnp.int32)
-    owner = jnp.sum(jnp.where(block_leaf[:, None] == positions[None, :], places[None, :], 0), axis=1)
-    order = jnp.arange(count, dtype=jnp.int32)
-    earlier = (owner[:, None] == owner[None, :]) & (order[None, :] < order[:, None])
-    slot = owner * capacity + jnp.sum(earlier.astype(jnp.int32), axis=1)
-    chosen = (jnp.arange(devices * capacity, dtype=jnp.int32)[:, None] == slot[None, :]).astype(BF16)
-    return jnp.dot(chosen, rows, preferred_element_type=F32).astype(BF16)
-
-
-def per_device(front_block, probe_right, probe_left, row_leaf, tree_leaf):
-    row_count = lax.axis_size("row")
-    col_count = lax.axis_size("col")
-    devices = row_count * col_count
-    row_index = lax.axis_index("row")
-    col_index = lax.axis_index("col")
+def iota(shape, axis):
+    return lax.broadcasted_iota(jnp.int32, shape, axis)
+
+
+def one_hot(condition):
+    return jnp.where(condition, 1.0, 0.0).astype(BF16)
+
+
+def column_of(row):
+    n = row.shape[1]
+    eye = one_hot(iota((n, n), 0) == iota((n, n), 1))
+    return mm(eye, jnp.broadcast_to(row, (n, n)).astype(BF16), ABT)
+
+
+def spread_matrix(leaf_row, tree_row, place_of_slot, slot_rank):
+    n = leaf_row.shape[1]
+    slots = place_of_slot.shape[0]
+    here = leaf_row.astype(F32)
+    twin = jnp.where((column_of(leaf_row) == here) & (iota((n, n), 0) < iota((n, n), 1)), 1.0, 0.0)
+    rank = jnp.sum(twin, axis=0, keepdims=True)
+    pick = one_hot(place_of_slot == iota((slots, n), 1))
+    named = mm(pick, jnp.broadcast_to(tree_row, (n, n)).astype(BF16), ABT)
+    return one_hot((named == here) & (slot_rank.astype(F32) == rank))
+
+
+def sample_kernel(
+    rows_n, cols_n, a_hbm, right_hbm, left_hbm, leaf_ref, tree_ref, s_out, u_out,
+    a_buf, right_buf, left_buf, off_buf, fs, fr, back, bs, bp, bsum, br,
+    f1s, f1r, f2s, f2r, b1s, b1r, b2s, b2r,
+    in_sem, fs_sem, fr_sem, ps_sem, pr_sem, bs_sem, br_sem,
+    f1s_sem, f1r_sem, f2s_sem, f2r_sem, b1s_sem, b1r_sem, b2s_sem, b2r_sem,
+):
+    i, j = lax.axis_index("row"), lax.axis_index("col")
+    lanes = fs.shape[1]
+    group = cols_n // 4
+    step_rows = group * lanes
+    y0 = j // group
+    x0, core = i // 2, i % 2
+    mesh_id = pl.DeviceIdType.MESH
+
+    def remote(src, dst, send_sem, recv_sem, device):
+        return pltpu.make_async_remote_copy(
+            src_ref=src, dst_ref=dst, send_sem=send_sem, recv_sem=recv_sem, device_id=device, device_id_type=mesh_id
+        )
+
+    barrier = pltpu.get_barrier_semaphore()
+
+    def greet_col(k, _):
+        pl.semaphore_signal(barrier, inc=1, device_id={"col": (j + k) % cols_n}, device_id_type=mesh_id)
+        return _
+
+    def greet_row(k, _):
+        pl.semaphore_signal(barrier, inc=1, device_id={"row": (i + k) % rows_n}, device_id_type=mesh_id)
+        return _
+
+    lax.fori_loop(1, cols_n, greet_col, 0)
+    lax.fori_loop(1, rows_n, greet_row, 0)
+
+    right_copy = pltpu.make_async_copy(right_hbm, right_buf, in_sem.at[4])
+    left_copy = pltpu.make_async_copy(left_hbm, left_buf, in_sem.at[5])
+
+    def rows_at(t):
+        return pl.ds(pl.multiple_of(((y0 + 1 + t) % 4) * step_rows, step_rows), step_rows)
+
+    def a_copy(t):
+        return pltpu.make_async_copy(a_hbm.at[rows_at(t)], a_buf.at[rows_at(t)], in_sem.at[t])
+
+    a_copy(0).start()
+    right_copy.start()
+    left_copy.start()
+    for t in range(1, 4):
+        a_copy(t).start()
+    back[...] = jnp.zeros_like(back)
+    right_copy.wait()
+    left_copy.wait()
+    pl.semaphore_wait(barrier, cols_n + rows_n - 2)
+    tiles = a_buf.shape[1] // lanes
+
+    def compute(t, carry):
+        a_copy(t).wait()
+        y = (y0 + 1 + t) % 4
+        base = pl.multiple_of(y * step_rows, step_rows)
+        for k in range(group):
+            mine = column_of(leaf_ref[pl.ds(i * cols_n + y * group + k, 1), :]).astype(BF16)
+            for c in range(tiles):
+                theirs = leaf_ref[pl.ds(j * rows_n + c, 1), :].astype(BF16)
+                block = a_buf[pl.ds(pl.multiple_of(base + k * lanes, lanes), lanes), c * lanes : (c + 1) * lanes]
+                off_buf[k * lanes : (k + 1) * lanes, c * lanes : (c + 1) * lanes] = jnp.where(
+                    mine == theirs, jnp.zeros_like(block), block
+                )
+        off = off_buf[...]
+        forward = mm(off, right_buf[...]).astype(BF16)
+        fs[pl.ds(y * group, group)] = forward.reshape(group, lanes, forward.shape[1])
+        for k in range(group):
+            peer = y * group + (j + k) % group
+
+            @pl.when(peer != j)
+            def _():
+                remote(fs.at[peer], fr.at[j], fs_sem.at[peer], fr_sem.at[j], {"col": peer}).start()
+
+        back[...] += mm(left_buf[pl.ds(base, step_rows), :], off, ATB)
+        return carry
+
+    lax.fori_loop(0, 4, compute, 0)
+    fr[pl.ds(j, 1)] = fs[pl.ds(j, 1)]
+
+    for k in range(rows_n):
+        bs[k % 2, k // 2] = back[:, k * lanes : (k + 1) * lanes]
+    other = 1 - core
+    chips = rows_n // 2
+
+    def pair(k):
+        x = (x0 + 1 + k) % chips
+        return x, remote(bs.at[other, x], bp.at[x], ps_sem.at[x], pr_sem.at[x], {"row": x0 * 2 + other})
+
+    def pair_start(k, carry):
+        pair(k)[1].start()
+        return carry
+
+    lax.fori_loop(0, chips, pair_start, 0)
+
+    def along(x):
+        return remote(bsum.at[x], br.at[x0], bs_sem.at[x], br_sem.at[x0], {"row": x * 2 + core})
+
+    def pair_end(k, carry):
+        x, copy = pair(k)
+        copy.wait()
+        bsum[pl.ds(x, 1)] = bs[core, pl.ds(x, 1)] + bp[pl.ds(x, 1)]
+
+        @pl.when(x != x0)
+        def _():
+            along(x).start()
+
+        return carry
+
+    lax.fori_loop(0, chips, pair_end, 0)
+
+    tree = tree_ref[...]
+    slots = s_out.shape[0]
+    slot = iota((slots, lanes), 0)
+    f_place = (slot // 2 % rows_n) * cols_n + slot // (2 * rows_n)
+    forward_map = spread_matrix(leaf_ref[pl.ds(i * cols_n + j, 1), :], tree, f_place, slot % 2)
+    backward_map = spread_matrix(leaf_ref[pl.ds(j * rows_n + i, 1), :], tree, slot // 2, slot % 2)
+
+    def along_end(k, carry):
+        x = (x0 + 1 + k) % chips
+        along(x).wait_send()
+        remote(bsum.at[x], br.at[x], bs_sem.at[x], br_sem.at[x], {"row": x * 2 + core}).wait_recv()
+        return carry
+
+    lax.fori_loop(0, chips - 1, along_end, 0)
+    br[pl.ds(x0, 1)] = bsum[pl.ds(x0, 1)]
+    sample_back = jnp.sum(br[...], axis=0).astype(BF16)
+    width = s_out.shape[1]
+
+    def rows_exchange(src, dst, send_sem, recv_sem):
+        def start(k, carry):
+            peer = (i + k) % rows_n
+            remote(src.at[peer], dst.at[i], send_sem.at[peer], recv_sem.at[i], {"row": peer}).start()
+            return carry
+
+        def end(k, carry):
+            peer = (i + k) % rows_n
+            remote(src.at[peer], dst.at[peer], send_sem.at[peer], recv_sem.at[peer], {"row": peer}).wait()
+            return carry
+
+        return start, end
+
+    def cols_exchange(src, dst, send_sem, recv_sem):
+        def start(k, carry):
+            peer = (j + k) % cols_n
+            remote(src.at[peer], dst.at[j], send_sem.at[peer], recv_sem.at[j], {"col": peer}).start()
+            return carry
+
+        def end(k, carry):
+            peer = (j + k) % cols_n
+            remote(src.at[peer], dst.at[peer], send_sem.at[peer], recv_sem.at[peer], {"col": peer}).wait()
+            return carry
+
+        return start, end
+
+    b1_start, b1_end = rows_exchange(b1s, b1r, b1s_sem, b1r_sem)
+    b2_start, b2_end = cols_exchange(b2s, b2r, b2s_sem, b2r_sem)
+    f1_start, f1_end = cols_exchange(f1s, f1r, f1s_sem, f1r_sem)
+    f2_start, f2_end = rows_exchange(f2s, f2r, f2s_sem, f2r_sem)
+    f0_end = cols_exchange(fs, fr, fs_sem, fr_sem)[1]
+
+    b1s[...] = mm(backward_map, sample_back, ABT).astype(BF16).reshape(b1s.shape)
+    lax.fori_loop(1, rows_n, b1_start, 0)
+    b1r[pl.ds(i, 1)] = b1s[pl.ds(i, 1)]
+
+    lax.fori_loop(1, cols_n, f0_end, 0)
+    forward_sum = fr[0].astype(F32)
+    for k in range(1, cols_n):
+        forward_sum += fr[k].astype(F32)
+    f1s[...] = mm(forward_map, forward_sum.astype(BF16)).astype(BF16).reshape(f1s.shape)
+    lax.fori_loop(1, cols_n, f1_start, 0)
+    f1r[pl.ds(j, 1)] = f1s[pl.ds(j, 1)]
+
+    slot = iota((slots, slots), 0)
+    source = iota((slots, slots), 1)
+    row_col = (slot // 2 % cols_n) * (2 * rows_n) + (slot // (2 * cols_n)) * 2 + slot % 2
+    col_row = (slot // 2 % rows_n) * (2 * cols_n) + (slot // (2 * rows_n)) * 2 + slot % 2
+    to_rows, to_cols = one_hot(source == row_col), one_hot(source == col_row)
+
+    lax.fori_loop(1, rows_n, b1_end, 0)
+    b2s[...] = mm(to_cols, b1r[...].reshape(slots, width)).astype(BF16).reshape(b2s.shape)
+    lax.fori_loop(1, cols_n, b2_start, 0)
+    b2r[pl.ds(j, 1)] = b2s[pl.ds(j, 1)]
+
+    lax.fori_loop(1, cols_n, f1_end, 0)
+    f2s[...] = mm(to_rows, f1r[...].reshape(slots, width)).astype(BF16).reshape(f2s.shape)
+    lax.fori_loop(1, rows_n, f2_start, 0)
+    f2r[pl.ds(i, 1)] = f2s[pl.ds(i, 1)]
+
+    lax.fori_loop(1, cols_n, b2_end, 0)
+    u_out[...] = b2r[...].reshape(slots, width)
+    lax.fori_loop(1, rows_n, f2_end, 0)
+    s_out[...] = f2r[...].reshape(slots, width)
+
+
+def sample_call(front_block, probe_right, probe_left, leaves, tree, rows_n, cols_n):
     tile_rows, tile_cols = front_block.shape
     samples = probe_right.shape[1]
-    leaves = row_leaf[:, 0]
-    rows_dev = leaves.shape[0] // devices
-    capacity = 2
-    rows_leaf = lax.dynamic_slice_in_dim(leaves, row_index * tile_rows, tile_rows)
-    cols_leaf = lax.dynamic_slice_in_dim(leaves, col_index * tile_cols, tile_cols)
-    same_leaf = rows_leaf[:, None] == cols_leaf[None, :]
-    off = jnp.where(same_leaf, jnp.zeros_like(front_block), front_block)
-    forward = jnp.dot(off, probe_right, preferred_element_type=F32).astype(BF16)
-    backward = lax.dot_general(off, probe_left, ATB, preferred_element_type=F32)
-    forward = lax.all_to_all(forward.reshape(col_count, rows_dev, samples), "col", 0, 0, tiled=True)
-    backward = lax.all_to_all(backward.reshape(row_count, rows_dev, samples), "row", 0, 0, tiled=True)
-    sample_rows = jnp.sum(forward.astype(F32), axis=0).astype(BF16)
-    sample_back = jnp.sum(backward, axis=0).astype(BF16)
-    positions = jnp.arange(devices, dtype=jnp.int32)
-    places = jnp.sum(jnp.where(tree_leaf[:, None] == positions[None, :], positions[:, None], 0), axis=0)
-
-    def block_leaf(block):
-        return lax.dynamic_slice_in_dim(leaves, block * rows_dev, rows_dev)
-
-    forward_send = spread(sample_rows, block_leaf(row_index * col_count + col_index), places, capacity, devices)
-    backward_send = spread(sample_back, block_leaf(col_index * row_count + row_index), places, capacity, devices)
-    both = jnp.stack(
-        [forward_send.reshape(devices, capacity, samples), backward_send.reshape(devices, capacity, samples)], axis=1
+    lanes = leaves.shape[1]
+    slots = 2 * rows_n * cols_n
+    chips = rows_n // 2
+    vmem = pl.BlockSpec(memory_space=pltpu.VMEM)
+    hbm = pl.BlockSpec(memory_space=pl.ANY)
+    out = jax.ShapeDtypeStruct((slots, samples), BF16)
+    by_col = pltpu.VMEM((cols_n, 2 * rows_n, samples), BF16)
+    by_row = pltpu.VMEM((rows_n, 2 * cols_n, samples), BF16)
+    dma = pltpu.SemaphoreType.DMA
+    return pl.pallas_call(
+        functools.partial(sample_kernel, rows_n, cols_n),
+        out_shape=(out, out),
+        in_specs=[hbm, hbm, hbm, vmem, vmem],
+        out_specs=(vmem, vmem),
+        scratch_shapes=[
+            pltpu.VMEM((tile_rows, tile_cols), BF16),
+            pltpu.VMEM((tile_cols, samples), BF16),
+            pltpu.VMEM((tile_rows, samples), BF16),
+            pltpu.VMEM((tile_rows // 4, tile_cols), BF16),
+            pltpu.VMEM((cols_n, lanes, samples), BF16),
+            pltpu.VMEM((cols_n, lanes, samples), BF16),
+            pltpu.VMEM((samples, tile_cols), F32),
+            pltpu.VMEM((2, chips, samples, lanes), F32),
+            pltpu.VMEM((chips, samples, lanes), F32),
+            pltpu.VMEM((chips, samples, lanes), F32),
+            pltpu.VMEM((chips, samples, lanes), F32),
+            by_col, by_col, by_row, by_row, by_row, by_row, by_col, by_col,
+            dma((6,)),
+            dma((cols_n,)), dma((cols_n,)),
+            dma((chips,)), dma((chips,)), dma((chips,)), dma((chips,)),
+            dma((cols_n,)), dma((cols_n,)), dma((rows_n,)), dma((rows_n,)),
+            dma((rows_n,)), dma((rows_n,)), dma((cols_n,)), dma((cols_n,)),
+        ],
+        compiler_params=pltpu.CompilerParams(collective_id=0, has_side_effects=True, vmem_limit_bytes=48 * 2**20),
+    )(front_block, probe_right, probe_left, leaves, tree)
+
+
+def per_device(front_block, probe_right, probe_left, row_leaf, tree_leaf):
+    rows_n, cols_n = lax.axis_size("row"), lax.axis_size("col")
+    devices = rows_n * cols_n
+    leaves = row_leaf.reshape(devices, row_leaf.shape[0] // devices)
+    forward_recv, backward_recv = sample_call(
+        front_block, probe_right, probe_left, leaves, tree_leaf.reshape(1, devices), rows_n, cols_n
     )
-    both = lax.all_to_all(both, ("row", "col"), split_axis=0, concat_axis=0, tiled=True)
-    forward_recv = both[:, 0].reshape(devices * capacity, samples)
-    backward_recv = both[:, 1].reshape(row_count, col_count, capacity, samples)
-    backward_recv = backward_recv.transpose(1, 0, 2, 3).reshape(devices * capacity, samples)
     coupling, sent = dense_call(leaf_kernel, forward_recv, backward_recv)
     merged = coupling
     for level in range(2):

time: 100 us -> 74.2 us (0.74)
  Pallas kernels: 15.8 us -> 53.2 us
  waiting for transfers between devices: 32.3 us -> 7.66 us
  blocking collectives: 17.4 us -> 0 us
  starting transfers between devices: 15.4 us -> 2.66 us
  matrix products: 9.95 us -> 0 us
  local copies, waits for them, and re-layouts: 5.33 us -> 8.54 us
  other arithmetic: 1.2 us -> 0 us
    pallas_call x0 -> x1, Pallas kernels: none -> 37.4 us  [sample_call(): pl.pallas_call(functools.partial(sample_kernel, rows_n, cols_n), out_shap...]
    all_to_all x2 -> x0, waiting for transfers between devices: 24.1 us -> none  [the longest x1 14.6 us: per_device(): lax.all_to_all(forward.reshape(col_count, rows_dev, samples), 'col', 0, 0...]
    all_to_all x1 -> x0, blocking collectives: 17.4 us -> none  [per_device(): lax.all_to_all(both, ('row', 'col'), split_axis=0, concat_axis=0, tiled=T...]
    all_to_all x2 -> x0, starting transfers between devices: 13.6 us -> none  [the longest x1 7.77 us: per_device(): lax.all_to_all(forward.reshape(col_count, rows_dev, samples), 'col', 0, 0...]
    dot_general x4 -> x0, matrix products: 9.95 us -> none  [the longest x1 4.93 us: per_device(): backward = lax.dot_general(off, probe_left, ATB, preferred_element_type=F32)]
    unnamed x11 -> x18, local copies, waits for them, and re-layouts: 1.35 us -> 8.54 us
    dynamic_slice x2 -> x0, local copies, waits for them, and re-layouts: 1.48 us -> none  [the longest x1 0.78 us: per_device(): lax.dynamic_slice_in_dim(leaves, col_index * tile_cols, tile_cols)]
  transfers between devices with their start and end apart: 4 -> 2, of which waited for: 4 -> 2; matrix products, arithmetic and copies ran while one was open for 6% -> 0% of each run, Pallas kernels for 0% -> 0%
where the time goes in v3:
time: 74.2 us; the launch traced here: 72.7 us
  Pallas kernels  53.2 us (72%)
  local copies, waits for them, and re-layouts  8.54 us (12%)
  waiting for transfers between devices  7.66 us (10%)
  starting transfers between devices  2.66 us (4%)
    pallas_call x1, Pallas kernels, sample_call(): pl.pallas_call(functools.partial(sample_kernel, rows_n, cols_n), out_shap...  37.4 us
    pallas_call x3, Pallas kernels, dense_call(): pl.pallas_call(kernel, out_shape=(jax.ShapeDtypeStruct((width, width), F3...  15.8 us
    unnamed x18, local copies, waits for them, and re-layouts  8.54 us
    ppermute x2, waiting for transfers between devices, from_partner(): return lax.ppermute(value, axis, pairs)  7.66 us
    ppermute x2, starting transfers between devices, from_partner(): return lax.ppermute(value, axis, pairs)  2.66 us
  transfers between devices with their start and end apart: 2, of which 2 were waited for; matrix products, arithmetic and copies ran while one was open for 0% of the time, Pallas kernels for 0%

profile of v3, /device:TPU:1, one launch (start us, length us, event | category | flops | bytes accessed | tf_op | source)
XLA Modules:
  0.0 72.7 jit_solution(20333742770164639)
XLA Ops:
  0.6 0.0 copy-start
  0.6 2.2 %copy-done = bf16[2048,1024]{1,0:T(8,128)(2,1)S(1)} copy-done((bf16[2048,1024]{1,0:T(8,128)(2,1)S(1)}, bf16[2048,1024]{1,0:T(8,128)(2,1)}, u32[]{:S(2)}) %copy-start) | copy-done | bytes 4194328
  2.8 0.0 copy-start.1
  2.8 1.2 %copy-done.1 = bf16[2048,256]{1,0:T(8,128)(2,1)S(1)} copy-done((bf16[2048,256]{1,0:T(8,128)(2,1)S(1)}, bf16[2048,256]{1,0:T(8,128)(2,1)}, u32[]{:S(2)}) %copy-start.1) | copy-done | bytes 1048600
  4.0 0.0 copy-start.2
  4.0 1.0 %copy-done.2 = bf16[1024,256]{1,0:T(8,128)(2,1)S(1)} copy-done((bf16[1024,256]{1,0:T(8,128)(2,1)S(1)}, bf16[1024,256]{1,0:T(8,128)(2,1)}, u32[]{:S(2)}) %copy-start.2) | copy-done | bytes 524312
  5.1 0.0 copy-start.5
  5.1 0.8 %copy-done.5 = s32[16384,1]{0,1:T(1,128)S(1)} copy-done((s32[16384,1]{0,1:T(1,128)S(1)}, s32[16384,1]{0,1:T(1,128)}, u32[]{:S(2)}) %copy-start.5) | copy-done | bytes 65560
  5.9 0.0 copy-start.6
  5.9 0.7 copy-done.6
  6.6 37.4 %shard_map.68 = (bf16[256,256]{1,0:T(8,128)(2,1)S(1)}, bf16[256,256]{1,0:T(8,128)(2,1)S(1)}) custom-call(bf16[2048,1024]{1,0:T(8,128)(2,1)S(1)} %copy-done, bf16[1024,256]{1,0:T(8,128)(2,1)S(1)} %copy-done.2, bf16[2048,256]{1,0:T(8,128)(2,1)S(1)} %copy-done.1, s32[128,128]{1,0:T(8,128)S(1)} %bitcast.4, s32[1,128]{1,0:T(1,128)S(1)} %bitcast.5), custom_call_target="tpu_custom_call" | custom-call | tf_op jit(solution)/shard_map/pallas_call | solution.py:366
  44.0 0.0 copy-start.3
  44.0 0.6 copy-done.3
  44.7 0.0 copy-start.4
  44.7 0.6 copy-done.4
  45.3 5.1 %shard_map.69 = (f32[256,256]{1,0:T(8,128)}, bf16[256,256]{1,0:T(8,128)(2,1)}) custom-call(bf16[256,256]{1,0:T(8,128)(2,1)} %copy-done.3, bf16[256,256]{1,0:T(8,128)(2,1)} %copy-done.4), custom_call_target="tpu_custom_call" | custom-call | tf_op jit(solution)/shard_map/pallas_call | solution.py:114
  50.4 0.9 %collective-permute-start = (bf16[256,256]{1,0:T(8,128)(2,1)}, bf16[256,256]{1,0:T(8,128)(2,1)S(1)}, u32[]{:S(2)}, u32[]{:S(2)}) collective-permute-start(bf16[256,256]{1,0:T(8,128)(2,1)} %get-tuple-element.12), channel_id=1, source_target_pairs={{0,1},{1,0},{2,3},{3,2},{4,5},{5,4},{6,7},{7,6},{8,9},{9,8},{10,11... | collective-permute-start | bytes 393224 | tf_op jit(solution)/shard_map/ppermute | solution.py:130
  51.4 3.9 %collective-permute-done.q_ref = bf16[256,256]{1,0:T(8,128)(2,1)S(1)} collective-permute-done((bf16[256,256]{1,0:T(8,128)(2,1)}, bf16[256,256]{1,0:T(8,128)(2,1)S(1)}, u32[]{:S(2)}, u32[]{:S(2)}) %collective-permute-start) | collective-permute-done | bytes 131104 | tf_op jit(solution)/shard_map/ppermute | solution.py:130
  55.2 0.0 copy-start.8
  55.2 0.7 copy-done.8
  55.9 5.3 %shard_map.70 = (f32[256,256]{1,0:T(8,128)}, bf16[256,256]{1,0:T(8,128)(2,1)}) custom-call(f32[256,256]{1,0:T(8,128)} %get-tuple-element.11.p_ref, bf16[256,256]{1,0:T(8,128)(2,1)} %copy-done.8), custom_call_target="tpu_custom_call" | custom-call | tf_op jit(solution)/shard_map/pallas_call | solution.py:114
  61.2 1.7 %collective-permute-start.1 = (bf16[256,256]{1,0:T(8,128)(2,1)}, bf16[256,256]{1,0:T(8,128)(2,1)S(1)}, u32[]{:S(2)}, u32[]{:S(2)}) collective-permute-start(bf16[256,256]{1,0:T(8,128)(2,1)} %get-tuple-element.14), channel_id=1, source_target_pairs={{0,2},{1,3},{2,0},{3,1},{4,6},{5,7},{6,4},{7,5},{8,10},{9,11},{10,... | collective-permute-start | bytes 393224 | tf_op jit(solution)/shard_map/ppermute | solution.py:130
  63.0 3.8 %collective-permute-done.1.q_ref = bf16[256,256]{1,0:T(8,128)(2,1)S(1)} collective-permute-done((bf16[256,256]{1,0:T(8,128)(2,1)}, bf16[256,256]{1,0:T(8,128)(2,1)S(1)}, u32[]{:S(2)}, u32[]{:S(2)}) %collective-permute-start.1) | collective-permute-done | bytes 131104 | tf_op jit(solution)/shard_map/ppermute | solution.py:130
  66.8 0.0 copy-start.7
  66.8 0.6 copy-done.7
  67.4 5.3 %shard_map.71 = (f32[256,256]{1,0:T(8,128)}, bf16[256,256]{1,0:T(8,128)(2,1)}) custom-call(f32[256,256]{1,0:T(8,128)} %get-tuple-element.13.p_ref, bf16[256,256]{1,0:T(8,128)(2,1)} %copy-done.7), custom_call_target="tpu_custom_call" | custom-call | tf_op jit(solution)/shard_map/pallas_call | solution.py:114
Async XLA Ops:
  0.6 2.2 %copy-start = (bf16[2048,1024]{1,0:T(8,128)(2,1)S(1)}, bf16[2048,1024]{1,0:T(8,128)(2,1)}, u32[]{:S(2)}) copy-start(bf16[2048,1024]{1,0:T(8,128)(2,1)} %a_hbm.1) | copy-start | bytes 12582916
  2.8 1.2 %copy-start.1 = (bf16[2048,256]{1,0:T(8,128)(2,1)S(1)}, bf16[2048,256]{1,0:T(8,128)(2,1)}, u32[]{:S(2)}) copy-start(bf16[2048,256]{1,0:T(8,128)(2,1)} %left_hbm.1) | copy-start | bytes 3145732
  4.0 1.0 %copy-start.2 = (bf16[1024,256]{1,0:T(8,128)(2,1)S(1)}, bf16[1024,256]{1,0:T(8,128)(2,1)}, u32[]{:S(2)}) copy-start(bf16[1024,256]{1,0:T(8,128)(2,1)} %right_hbm.1) | copy-start | bytes 1572868
  5.1 0.8 %copy-start.5 = (s32[16384,1]{0,1:T(1,128)S(1)}, s32[16384,1]{0,1:T(1,128)}, u32[]{:S(2)}) copy-start(s32[16384,1]{0,1:T(1,128)} %param.8) | copy-start | bytes 196612
  5.9 0.7 copy-start.6
  44.0 0.7 copy-start.3
  44.7 0.6 copy-start.4
  50.4 4.8 %collective-permute-start = (bf16[256,256]{1,0:T(8,128)(2,1)}, bf16[256,256]{1,0:T(8,128)(2,1)S(1)}, u32[]{:S(2)}, u32[]{:S(2)}) collective-permute-start(bf16[256,256]{1,0:T(8,128)(2,1)} %get-tuple-element.12), channel_id=1, source_target_pairs={{0,1},{1,0},{2,3},{3,2},{4,5},{5,4},{6,7},{7,6},{8,9},{9,8},{10,11... | collective-permute-start | bytes 393224 | tf_op jit(solution)/shard_map/ppermute | solution.py:130
  55.2 0.7 copy-start.8
  61.2 5.5 %collective-permute-start.1 = (bf16[256,256]{1,0:T(8,128)(2,1)}, bf16[256,256]{1,0:T(8,128)(2,1)S(1)}, u32[]{:S(2)}, u32[]{:S(2)}) collective-permute-start(bf16[256,256]{1,0:T(8,128)(2,1)} %get-tuple-element.14), channel_id=1, source_target_pairs={{0,2},{1,3},{2,0},{3,1},{4,6},{5,7},{6,4},{7,5},{8,10},{9,11},{10,... | collective-permute-start | bytes 393224 | tf_op jit(solution)/shard_map/ppermute | solution.py:130
  66.8 0.7 copy-start.7

commit v4 on v3

--- a/solution.py
+++ b/solution.py
@@ -27,8 +27,8 @@
     return mm(left[0], right[0], dims) + (mm(left[0], right[1], dims) + mm(left[1], right[0], dims))
 
 
-def whiten(gram, squares, cross, out_ref, send_ref, b_ref, x_ref, g_ref):
-    width = gram.shape[0]
+def whiten(problems, b_ref, x_ref, g_ref):
+    width = problems[0][0].shape[0]
     row = lax.broadcasted_iota(jnp.int32, (width, width), 0)
     col = lax.broadcasted_iota(jnp.int32, (width, width), 1)
     below, diag = row > col, row == col
@@ -39,93 +39,123 @@
     def factor(value):
         return jnp.where(below, -value, jnp.where(diag, 1.5 - 0.5 * value, 0.0)).astype(BF16)
 
-    ridge = squares / width + eps
-    inv_root = lax.rsqrt(ridge)
-    unit = gram * (inv_root * inv_root) + diag.astype(F32)
-    g_high, g_low = split(unit)
-    g_ref[0] = g_high
-    g_ref[1] = g_low
-    rhs = split(cross * inv_root)
-    square = mm(g_high, g_high)
-    fourth = jnp.sum(jnp.sum(square * square, axis=1, keepdims=True), axis=0, keepdims=True)
-    scale = 0.99 * lax.rsqrt(jnp.sqrt(fourth))
-    fourth_scalar = jnp.sum(fourth)
-    steps = jnp.int32(3)
-    for k in range(1, 8):
-        steps = steps + (fourth_scalar > 2.25 ** (4 * k)).astype(jnp.int32)
-    extra = (fourth_scalar > 48.0**4).astype(jnp.int32)
-
-    b0 = unit * scale
-    t0 = factor(b0)
-    b_ref[...] = mm(mm(t0, b0.astype(BF16)).astype(BF16), t0, ABT)
-    x_ref[...] = t0.astype(F32) * jnp.sqrt(scale)
-
-    def step(_, carry):
-        b = b_ref[...]
+    def step(b, x, growth):
+        b = b * growth
         t = factor(b)
         y = mm(t, b.astype(BF16))
-        x = mm(t, x_ref[...].astype(BF16))
-        b_ref[...] = mm(y.astype(BF16), t, ABT)
-        x_ref[...] = x
-        return carry
-
-    lax.fori_loop(1, steps, step, 0)
-
-    def error(x):
-        y = split(mm3(x, (g_ref[0], g_ref[1])))
+        return mm(y.astype(BF16), t, ABT), mm(t, (x * growth**0.5).astype(BF16))
+
+    def error(x, n):
+        y = split(mm3(x, (g_ref[n, 0], g_ref[n, 1])))
         return half(mm3(y, x, ABT) - diag.astype(F32))
 
+    rhs, worst, states = [], None, []
+    for n, (gram, squares, cross) in enumerate(problems):
+        ridge = squares / width + eps
+        inv_root = lax.rsqrt(ridge)
+        unit = gram * (inv_root * inv_root) + diag.astype(F32)
+        g_ref[n, 0], g_ref[n, 1] = split(unit)
+        rhs.append(split(cross * inv_root))
+        high = unit.astype(BF16)
+        square = mm(high, high)
+        fourth = total(square * square)
+        worst = fourth if worst is None else jnp.maximum(worst, fourth)
+        scale = 1.9 * lax.rsqrt(jnp.sqrt(fourth))
+        b = unit * scale
+        t = factor(b)
+        states.append((mm(mm(t, b.astype(BF16)).astype(BF16), t, ABT), t.astype(F32) * jnp.sqrt(scale)))
+    worst = jnp.sum(worst)
+    steps = jnp.int32(4)
+    for bound in (20.0, 45.0, 100.0, 180.0):
+        steps = steps + (worst > bound**4).astype(jnp.int32)
+    extra = (worst > 48.0**4).astype(jnp.int32)
+
+    for growth in (1.3, 1.2, 1.0):
+        states = [step(b, x, growth) for b, x in states]
+    for n, (b, x) in enumerate(states):
+        b_ref[n] = b
+        x_ref[n] = x
+
+    def more(_, carry):
+        for n in range(len(problems)):
+            b_ref[n], x_ref[n] = step(b_ref[n], x_ref[n], 1.0)
+        return carry
+
     def fix(_, carry):
-        x = split(x_ref[...])
-        x_ref[...] = x_ref[...] - mm3(split(error(x)), x)
-        return carry
-
+        for n in range(len(problems)):
+            x = split(x_ref[n])
+            x_ref[n] = x_ref[n] - mm3(split(error(x, n)), x)
+        return carry
+
+    lax.fori_loop(4, steps, more, 0)
     lax.fori_loop(0, extra, fix, 0)
-    x = split(x_ref[...])
-    z = mm3(x, rhs)
-    out = z - mm(error(x).astype(BF16), z.astype(BF16))
+    outs = []
+    for n in range(len(problems)):
+        x = split(x_ref[n])
+        z = mm3(x, rhs[n])
+        outs.append(z - mm(error(x, n).astype(BF16), z.astype(BF16)))
+    return outs
+
+
+def total(value):
+    return jnp.sum(jnp.sum(value, axis=1, keepdims=True), axis=0, keepdims=True)
+
+
+def leaf_kernel(s_ref, u_ref, out_ref, send_ref, *refs):
+    s, u = s_ref[...], u_ref[...]
+    wide = s.astype(F32)
+    (out,) = whiten([(mm(s, s, ATB), total(wide * wide), mm(s, u, ATB))], *refs)
     out_ref[...] = out
     send_ref[...] = out.astype(BF16)
 
 
-def total(value):
-    return jnp.sum(jnp.sum(value, axis=1, keepdims=True), axis=0, keepdims=True)
-
-
-def leaf_kernel(s_ref, u_ref, out_ref, *refs):
-    s, u = s_ref[...], u_ref[...]
-    wide = s.astype(F32)
-    whiten(mm(s, s, ATB), total(wide * wide), mm(s, u, ATB), out_ref, *refs)
-
-
-def merge_kernel(p_ref, q_ref, out_ref, *refs):
-    p, q = p_ref[...], q_ref[...]
-    wide = q.astype(F32)
-    squares = total(p * p + wide * wide)
-    high, low = split(p)
-    gram = mm3((high, low), (high, low), ATB) + mm(q, q, ATB)
-    cross = mm(high, q, ATB) + mm(low, q, ATB)
-    whiten(gram, squares, cross + cross.T, out_ref, *refs)
-
-
-def dense_call(kernel, left, right):
-    width = left.shape[1]
+def merge_parts(p, q):
+    gram, squares = 0.0, 0.0
+    for high, low in (p, q):
+        if low is None:
+            wide = high.astype(F32)
+            gram += mm(high, high, ATB)
+        else:
+            wide = high.astype(F32) + low.astype(F32)
+            gram += mm3((high, low), (high, low), ATB)
+        squares += total(wide * wide)
+    cross = mm(p[0], q[0], ATB)
+    if p[1] is not None:
+        cross += mm(p[1], q[0], ATB)
+    if q[1] is not None:
+        cross += mm(p[0], q[1], ATB)
+    return gram, squares, cross + cross.T
+
+
+def merge_kernel(p_ref, q1_ref, q2_ref, q3_ref, out_ref, *refs):
+    near, far = whiten(
+        [
+            merge_parts(split(p_ref[...]), (q1_ref[...], None)),
+            merge_parts((q2_ref[...], None), (q3_ref[...], None)),
+        ],
+        *refs,
+    )
+    (out_ref[...],) = whiten([merge_parts(split(near), split(far))], *refs)
+
+
+def dense_call(kernel, out_shapes, problems, *args):
+    width = args[0].shape[1]
     whole = pl.BlockSpec(memory_space=pltpu.VMEM)
     return pl.pallas_call(
         kernel,
-        out_shape=(jax.ShapeDtypeStruct((width, width), F32), jax.ShapeDtypeStruct((width, width), BF16)),
-        in_specs=[whole, whole],
-        out_specs=(whole, whole),
+        out_shape=tuple(jax.ShapeDtypeStruct((width, width), dtype) for dtype in out_shapes),
+        in_specs=[whole] * len(args),
+        out_specs=(whole,) * len(out_shapes),
         scratch_shapes=[
-            pltpu.VMEM((width, width), F32),
-            pltpu.VMEM((width, width), F32),
-            pltpu.VMEM((2, width, width), BF16),
+            pltpu.VMEM((problems, width, width), F32),
+            pltpu.VMEM((problems, width, width), F32),
+            pltpu.VMEM((problems, 2, width, width), BF16),
         ],
-    )(left, right)
-
-
-def from_partner(value, axis, distance):
-    mask = 2**distance
+        compiler_params=pltpu.CompilerParams(vmem_limit_bytes=16 * 2**20),
+    )(*args)
+
+
+def from_partner(value, axis, mask):
     pairs = [(source, source ^ mask) for source in range(lax.axis_size(axis))]
     return lax.ppermute(value, axis, pairs)
 
@@ -156,8 +186,8 @@
 
 
 def sample_kernel(
-    rows_n, cols_n, a_hbm, right_hbm, left_hbm, leaf_ref, tree_ref, s_out, u_out,
-    a_buf, right_buf, left_buf, off_buf, fs, fr, back, bs, bp, bsum, br,
+    rows_n, cols_n, a_hbm, right_hbm, left_hbm, leaf_hbm, tree_hbm, s_out, u_out,
+    leaf_ref, tree_ref, a_buf, right_buf, left_buf, fs, fr, back, bs, bp, bsum, br,
     f1s, f1r, f2s, f2r, b1s, b1r, b2s, b2r,
     in_sem, fs_sem, fr_sem, ps_sem, pr_sem, bs_sem, br_sem,
     f1s_sem, f1r_sem, f2s_sem, f2r_sem, b1s_sem, b1r_sem, b2s_sem, b2r_sem,
@@ -190,6 +220,8 @@
 
     right_copy = pltpu.make_async_copy(right_hbm, right_buf, in_sem.at[4])
     left_copy = pltpu.make_async_copy(left_hbm, left_buf, in_sem.at[5])
+    leaf_copy = pltpu.make_async_copy(leaf_hbm, leaf_ref, in_sem.at[6])
+    tree_copy = pltpu.make_async_copy(tree_hbm, tree_ref, in_sem.at[7])
 
     def rows_at(t):
         return pl.ds(pl.multiple_of(((y0 + 1 + t) % 4) * step_rows, step_rows), step_rows)
@@ -197,31 +229,55 @@
     def a_copy(t):
         return pltpu.make_async_copy(a_hbm.at[rows_at(t)], a_buf.at[rows_at(t)], in_sem.at[t])
 
-    a_copy(0).start()
+    leaf_copy.start()
+    tree_copy.start()
+    left_copy.start()
+    for t in range(4):
+        a_copy(t).start()
     right_copy.start()
-    left_copy.start()
-    for t in range(1, 4):
-        a_copy(t).start()
-    back[...] = jnp.zeros_like(back)
+    leaf_copy.wait()
+    tree_copy.wait()
+    tiles = a_buf.shape[1] // lanes
+    for t in range(4):
+        a_copy(t).wait()
+        if t == 0:
+            left_copy.wait()
+        base = pl.multiple_of(((y0 + 1 + t) % 4) * step_rows, step_rows)
+        for k in range(group):
+            mine = column_of(leaf_ref[pl.ds(i * cols_n + base // lanes + k, 1), :]).astype(BF16)
+            rows = pl.ds(pl.multiple_of(base + k * lanes, lanes), lanes)
+            for c in range(tiles):
+                theirs = leaf_ref[pl.ds(j * rows_n + c, 1), :].astype(BF16)
+                block = a_buf[rows, c * lanes : (c + 1) * lanes]
+                a_buf[rows, c * lanes : (c + 1) * lanes] = jnp.where(mine == theirs, jnp.zeros_like(block), block)
+        part = mm(left_buf[pl.ds(base, step_rows), :], a_buf[pl.ds(base, step_rows), :], ATB)
+        if t == 0:
+            back[...] = part
+        elif t < 3:
+            back[...] += part
+        else:
+            part += back[...]
+            for k in range(rows_n):
+                bs[k % 2, k // 2] = part[:, k * lanes : (k + 1) * lanes]
+    pl.semaphore_wait(barrier, cols_n + rows_n - 2)
+    other = 1 - core
+    chips = rows_n // 2
+
+    def pair(k):
+        x = (x0 + 1 + k) % chips
+        return x, remote(bs.at[other, x], bp.at[x], ps_sem.at[x], pr_sem.at[x], {"row": x0 * 2 + other})
+
+    def pair_start(k, carry):
+        pair(k)[1].start()
+        return carry
+
+    lax.fori_loop(0, chips, pair_start, 0)
     right_copy.wait()
-    left_copy.wait()
-    pl.semaphore_wait(barrier, cols_n + rows_n - 2)
-    tiles = a_buf.shape[1] // lanes
 
     def compute(t, carry):
-        a_copy(t).wait()
         y = (y0 + 1 + t) % 4
         base = pl.multiple_of(y * step_rows, step_rows)
-        for k in range(group):
-            mine = column_of(leaf_ref[pl.ds(i * cols_n + y * group + k, 1), :]).astype(BF16)
-            for c in range(tiles):
-                theirs = leaf_ref[pl.ds(j * rows_n + c, 1), :].astype(BF16)
-                block = a_buf[pl.ds(pl.multiple_of(base + k * lanes, lanes), lanes), c * lanes : (c + 1) * lanes]
-                off_buf[k * lanes : (k + 1) * lanes, c * lanes : (c + 1) * lanes] = jnp.where(
-                    mine == theirs, jnp.zeros_like(block), block
-                )
-        off = off_buf[...]
-        forward = mm(off, right_buf[...]).astype(BF16)
+        forward = mm(a_buf[pl.ds(base, step_rows), :], right_buf[...]).astype(BF16)
         fs[pl.ds(y * group, group)] = forward.reshape(group, lanes, forward.shape[1])
         for k in range(group):
             peer = y * group + (j + k) % group
@@ -230,26 +286,10 @@
             def _():
                 remote(fs.at[peer], fr.at[j], fs_sem.at[peer], fr_sem.at[j], {"col": peer}).start()
 
-        back[...] += mm(left_buf[pl.ds(base, step_rows), :], off, ATB)
         return carry
 
     lax.fori_loop(0, 4, compute, 0)
     fr[pl.ds(j, 1)] = fs[pl.ds(j, 1)]
-
-    for k in range(rows_n):
-        bs[k % 2, k // 2] = back[:, k * lanes : (k + 1) * lanes]
-    other = 1 - core
-    chips = rows_n // 2
-
-    def pair(k):
-        x = (x0 + 1 + k) % chips
-        return x, remote(bs.at[other, x], bp.at[x], ps_sem.at[x], pr_sem.at[x], {"row": x0 * 2 + other})
-
-    def pair_start(k, carry):
-        pair(k)[1].start()
-        return carry
-
-    lax.fori_loop(0, chips, pair_start, 0)
 
     def along(x):
         return remote(bsum.at[x], br.at[x0], bs_sem.at[x], br_sem.at[x0], {"row": x * 2 + core})
@@ -270,9 +310,10 @@
     tree = tree_ref[...]
     slots = s_out.shape[0]
     slot = iota((slots, lanes), 0)
-    f_place = (slot // 2 % rows_n) * cols_n + slot // (2 * rows_n)
-    forward_map = spread_matrix(leaf_ref[pl.ds(i * cols_n + j, 1), :], tree, f_place, slot % 2)
-    backward_map = spread_matrix(leaf_ref[pl.ds(j * rows_n + i, 1), :], tree, slot // 2, slot % 2)
+    row_bits, col_bits = rows_n.bit_length() - 1, cols_n.bit_length() - 1
+    f_place = (((slot >> 1) & (rows_n - 1)) << col_bits) + (slot >> (1 + row_bits))
+    forward_map = spread_matrix(leaf_ref[pl.ds(i * cols_n + j, 1), :], tree, f_place, slot & 1)
+    backward_map = spread_matrix(leaf_ref[pl.ds(j * rows_n + i, 1), :], tree, slot >> 1, slot & 1)
 
     def along_end(k, carry):
         x = (x0 + 1 + k) % chips
@@ -331,8 +372,8 @@
 
     slot = iota((slots, slots), 0)
     source = iota((slots, slots), 1)
-    row_col = (slot // 2 % cols_n) * (2 * rows_n) + (slot // (2 * cols_n)) * 2 + slot % 2
-    col_row = (slot // 2 % rows_n) * (2 * cols_n) + (slot // (2 * rows_n)) * 2 + slot % 2
+    row_col = (((slot >> 1) & (cols_n - 1)) << (1 + row_bits)) + ((slot >> (1 + col_bits)) << 1) + (slot & 1)
+    col_row = (((slot >> 1) & (rows_n - 1)) << (1 + col_bits)) + ((slot >> (1 + row_bits)) << 1) + (slot & 1)
     to_rows, to_cols = one_hot(source == row_col), one_hot(source == col_row)
 
     lax.fori_loop(1, rows_n, b1_end, 0)
@@ -358,7 +399,7 @@
     slots = 2 * rows_n * cols_n
     chips = rows_n // 2
     vmem = pl.BlockSpec(memory_space=pltpu.VMEM)
-    hbm = pl.BlockSpec(memory_space=pl.ANY)
+    hbm = pl.BlockSpec(memory_space=pltpu.HBM)
     out = jax.ShapeDtypeStruct((slots, samples), BF16)
     by_col = pltpu.VMEM((cols_n, 2 * rows_n, samples), BF16)
     by_row = pltpu.VMEM((rows_n, 2 * cols_n, samples), BF16)
@@ -366,13 +407,14 @@
     return pl.pallas_call(
         functools.partial(sample_kernel, rows_n, cols_n),
         out_shape=(out, out),
-        in_specs=[hbm, hbm, hbm, vmem, vmem],
+        in_specs=[hbm] * 5,
         out_specs=(vmem, vmem),
         scratch_shapes=[
+            pltpu.VMEM(leaves.shape, jnp.int32),
+            pltpu.VMEM(tree.shape, jnp.int32),
             pltpu.VMEM((tile_rows, tile_cols), BF16),
             pltpu.VMEM((tile_cols, samples), BF16),
             pltpu.VMEM((tile_rows, samples), BF16),
-            pltpu.VMEM((tile_rows // 4, tile_cols), BF16),
             pltpu.VMEM((cols_n, lanes, samples), BF16),
             pltpu.VMEM((cols_n, lanes, samples), BF16),
             pltpu.VMEM((samples, tile_cols), F32),
@@ -381,13 +423,13 @@
             pltpu.VMEM((chips, samples, lanes), F32),
             pltpu.VMEM((chips, samples, lanes), F32),
             by_col, by_col, by_row, by_row, by_row, by_row, by_col, by_col,
-            dma((6,)),
+            dma((8,)),
             dma((cols_n,)), dma((cols_n,)),
             dma((chips,)), dma((chips,)), dma((chips,)), dma((chips,)),
             dma((cols_n,)), dma((cols_n,)), dma((rows_n,)), dma((rows_n,)),
             dma((rows_n,)), dma((rows_n,)), dma((cols_n,)), dma((cols_n,)),
         ],
-        compiler_params=pltpu.CompilerParams(collective_id=0, has_side_effects=True, vmem_limit_bytes=48 * 2**20),
+        compiler_params=pltpu.CompilerParams(collective_id=0, has_side_effects=True, vmem_limit_bytes=67043328),
     )(front_block, probe_right, probe_left, leaves, tree)
 
 
@@ -398,10 +440,9 @@
     forward_recv, backward_recv = sample_call(
         front_block, probe_right, probe_left, leaves, tree_leaf.reshape(1, devices), rows_n, cols_n
     )
-    coupling, sent = dense_call(leaf_kernel, forward_recv, backward_recv)
-    merged = coupling
-    for level in range(2):
-        merged, sent = dense_call(merge_kernel, merged, from_partner(sent, "col", level))
+    coupling, sent = dense_call(leaf_kernel, (F32, BF16), 1, forward_recv, backward_recv)
+    others = [from_partner(sent, "col", mask) for mask in (1, 2, 3)]
+    (merged,) = dense_call(merge_kernel, (F32,), 2, coupling, *others)
     return (coupling[None], merged[None])
 
 

time: 74.2 us -> 64 us (0.86); the launches traced: 72.7 us -> 63.7 us
  local copies, waits for them, and re-layouts: 8.54 us -> 2.75 us
  Pallas kernels: 53.2 us -> 51.2 us
  waiting for transfers between devices: 7.66 us -> 5.8 us
    unnamed x18 -> x6, local copies, waits for them, and re-layouts: 8.54 us -> 2.75 us
    pallas_call x3 -> x2, Pallas kernels: 15.8 us -> 12.2 us  [dense_call(): pl.pallas_call(kernel, out_shape=tuple((jax.ShapeDtypeStruct((width, widt...]
    ppermute x2 -> x3, waiting for transfers between devices: 7.66 us -> 5.8 us  [from_partner(): return lax.ppermute(value, axis, pairs)]
    pallas_call x1, Pallas kernels: 37.4 us -> 39.1 us  [sample_call(): pl.pallas_call(functools.partial(sample_kernel, rows_n, cols_n), out_shap...]
    ppermute x2 -> x3, starting transfers between devices: 2.66 us -> 3.25 us  [from_partner(): return lax.ppermute(value, axis, pairs)]
  transfers between devices with their start and end apart: 2 -> 3, of which waited for: 2 -> 3; matrix products, arithmetic and copies ran while one was open for 0% -> 0% of each run, Pallas kernels for 0% -> 0%
where the time goes in v4:
time: 64 us; the launch traced here: 63.7 us
  Pallas kernels  51.2 us (80%)
  waiting for transfers between devices  5.8 us (9%)
  starting transfers between devices  3.25 us (5%)
  local copies, waits for them, and re-layouts  2.75 us (4%)
  between operations  0.65 us (1%)
    pallas_call x1, Pallas kernels, sample_call(): pl.pallas_call(functools.partial(sample_kernel, rows_n, cols_n), out_shap...  39.1 us
    pallas_call x2, Pallas kernels, dense_call(): pl.pallas_call(kernel, out_shape=tuple((jax.ShapeDtypeStruct((width, widt...  12.2 us
    ppermute x3, waiting for transfers between devices, from_partner(): return lax.ppermute(value, axis, pairs)  5.8 us
    ppermute x3, starting transfers between devices, from_partner(): return lax.ppermute(value, axis, pairs)  3.25 us
    unnamed x6, local copies, waits for them, and re-layouts  2.75 us
  transfers between devices with their start and end apart: 3, of which 3 were waited for; matrix products, arithmetic and copies ran while one was open for 0% of the time, Pallas kernels for 0%

profile of v4, /device:TPU:1, one launch (start us, length us, event | category | flops | bytes accessed | tf_op | source)
XLA Modules:
  0.0 63.7 jit_solution(7863043929101939525)
XLA Ops:
  0.6 39.1 %shard_map.68 = (bf16[256,256]{1,0:T(8,128)(2,1)}, bf16[256,256]{1,0:T(8,128)(2,1)}) custom-call(bf16[2048,1024]{1,0:T(8,128)(2,1)} %a_hbm.1, bf16[1024,256]{1,0:T(8,128)(2,1)} %right_hbm.1, bf16[2048,256]{1,0:T(8,128)(2,1)} %left_hbm.1, s32[128,128]{1,0:T(8,128)} %bitcast.6, s32[1,128]{1,0:T(1,128)} %bitcast.7), custom_call_target="tpu_custom_call" | custom-call | tf_op jit(solution)/shard_map/pallas_call | solution.py:407
  39.7 0.0 copy-start.1
  39.7 0.9 %copy-done.1 = bf16[256,256]{1,0:T(8,128)(2,1)S(1)} copy-done((bf16[256,256]{1,0:T(8,128)(2,1)S(1)}, bf16[256,256]{1,0:T(8,128)(2,1)}, u32[]{:S(2)}) %copy-start.1) | copy-done | bytes 131096
  40.6 0.0 copy-start.2
  40.6 0.9 %copy-done.2 = bf16[256,256]{1,0:T(8,128)(2,1)S(1)} copy-done((bf16[256,256]{1,0:T(8,128)(2,1)S(1)}, bf16[256,256]{1,0:T(8,128)(2,1)}, u32[]{:S(2)}) %copy-start.2) | copy-done | bytes 131096
  41.5 3.7 %shard_map.69 = (f32[256,256]{1,0:T(8,128)}, bf16[256,256]{1,0:T(8,128)(2,1)S(1)}) custom-call(bf16[256,256]{1,0:T(8,128)(2,1)S(1)} %copy-done.1, bf16[256,256]{1,0:T(8,128)(2,1)S(1)} %copy-done.2), custom_call_target="tpu_custom_call" | custom-call | tf_op jit(solution)/shard_map/pallas_call | solution.py:144
  45.2 1.6 %collective-permute-start.2 = (bf16[256,256]{1,0:T(8,128)(2,1)S(1)}, bf16[256,256]{1,0:T(8,128)(2,1)S(1)}, u32[]{:S(2)}, u32[]{:S(2)}) collective-permute-start(bf16[256,256]{1,0:T(8,128)(2,1)S(1)} %get-tuple-element.9), channel_id=1, source_target_pairs={{0,3},{1,2},{2,1},{3,0},{4,7},{5,6},{6,5},{7,4},{8,11},{9,10},{10,... | collective-permute-start | bytes 393224 | tf_op jit(solution)/shard_map/ppermute | solution.py:160
  46.8 0.0 collective-permute-start.1
  46.8 1.7 %collective-permute-start = (bf16[256,256]{1,0:T(8,128)(2,1)S(1)}, bf16[256,256]{1,0:T(8,128)(2,1)S(1)}, u32[]{:S(2)}, u32[]{:S(2)}) collective-permute-start(bf16[256,256]{1,0:T(8,128)(2,1)S(1)} %get-tuple-element.9), channel_id=1, source_target_pairs={{0,1},{1,0},{2,3},{3,2},{4,5},{5,4},{6,7},{7,6},{8,9},{9,8},{10,11... | collective-permute-start | bytes 393224 | tf_op jit(solution)/shard_map/ppermute | solution.py:160
  48.4 2.6 %collective-permute-done.2.q3_ref = bf16[256,256]{1,0:T(8,128)(2,1)S(1)} collective-permute-done((bf16[256,256]{1,0:T(8,128)(2,1)S(1)}, bf16[256,256]{1,0:T(8,128)(2,1)S(1)}, u32[]{:S(2)}, u32[]{:S(2)}) %collective-permute-start.2) | collective-permute-done | bytes 131104 | tf_op jit(solution)/shard_map/ppermute | solution.py:160
  51.1 1.7 %collective-permute-done.1.q2_ref = bf16[256,256]{1,0:T(8,128)(2,1)S(1)} collective-permute-done((bf16[256,256]{1,0:T(8,128)(2,1)S(1)}, bf16[256,256]{1,0:T(8,128)(2,1)S(1)}, u32[]{:S(2)}, u32[]{:S(2)}) %collective-permute-start.1) | collective-permute-done | bytes 131104 | tf_op jit(solution)/shard_map/ppermute | solution.py:160
  52.8 1.5 %collective-permute-done.q1_ref = bf16[256,256]{1,0:T(8,128)(2,1)S(1)} collective-permute-done((bf16[256,256]{1,0:T(8,128)(2,1)S(1)}, bf16[256,256]{1,0:T(8,128)(2,1)S(1)}, u32[]{:S(2)}, u32[]{:S(2)}) %collective-permute-start) | collective-permute-done | bytes 131104 | tf_op jit(solution)/shard_map/ppermute | solution.py:160
  54.3 0.0 copy-start
  54.3 0.9 %copy-done = f32[256,256]{1,0:T(8,128)S(1)} copy-done((f32[256,256]{1,0:T(8,128)S(1)}, f32[256,256]{1,0:T(8,128)}, u32[]{:S(2)}) %copy-start) | copy-done | bytes 262168
  55.2 8.5 %shard_map.70 = f32[256,256]{1,0:T(8,128)} custom-call(f32[256,256]{1,0:T(8,128)S(1)} %copy-done, bf16[256,256]{1,0:T(8,128)(2,1)S(1)} %collective-permute-done.q1_ref, bf16[256,256]{1,0:T(8,128)(2,1)S(1)} %collective-permute-done.1.q2_ref, bf16[256,256]{1,0:T(8,128)(2,1)S(1)} %collective-permute-done.2.q3_ref), custom_call_target="tpu_custom_call" | custom-call | tf_op jit(solution)/shard_map/pallas_call | solution.py:144
Async XLA Ops:
  39.7 0.9 %copy-start.1 = (bf16[256,256]{1,0:T(8,128)(2,1)S(1)}, bf16[256,256]{1,0:T(8,128)(2,1)}, u32[]{:S(2)}) copy-start(bf16[256,256]{1,0:T(8,128)(2,1)} %get-tuple-element.6.s_ref) | copy-start | bytes 393220
  40.6 0.9 %copy-start.2 = (bf16[256,256]{1,0:T(8,128)(2,1)S(1)}, bf16[256,256]{1,0:T(8,128)(2,1)}, u32[]{:S(2)}) copy-start(bf16[256,256]{1,0:T(8,128)(2,1)} %get-tuple-element.7.u_ref) | copy-start | bytes 393220
  45.2 5.9 %collective-permute-start.2 = (bf16[256,256]{1,0:T(8,128)(2,1)S(1)}, bf16[256,256]{1,0:T(8,128)(2,1)S(1)}, u32[]{:S(2)}, u32[]{:S(2)}) collective-permute-start(bf16[256,256]{1,0:T(8,128)(2,1)S(1)} %get-tuple-element.9), channel_id=1, source_target_pairs={{0,3},{1,2},{2,1},{3,0},{4,7},{5,6},{6,5},{7,4},{8,11},{9,10},{10,... | collective-permute-start | bytes 393224 | tf_op jit(solution)/shard_map/ppermute | solution.py:160
  46.8 6.0 %collective-permute-start.1 = (bf16[256,256]{1,0:T(8,128)(2,1)S(1)}, bf16[256,256]{1,0:T(8,128)(2,1)S(1)}, u32[]{:S(2)}, u32[]{:S(2)}) collective-permute-start(bf16[256,256]{1,0:T(8,128)(2,1)S(1)} %get-tuple-element.9), channel_id=1, source_target_pairs={{0,2},{1,3},{2,0},{3,1},{4,6},{5,7},{6,4},{7,5},{8,10},{9,11},{10,... | collective-permute-start | bytes 393224 | tf_op jit(solution)/shard_map/ppermute | solution.py:160
  46.8 7.5 %collective-permute-start = (bf16[256,256]{1,0:T(8,128)(2,1)S(1)}, bf16[256,256]{1,0:T(8,128)(2,1)S(1)}, u32[]{:S(2)}, u32[]{:S(2)}) collective-permute-start(bf16[256,256]{1,0:T(8,128)(2,1)S(1)} %get-tuple-element.9), channel_id=1, source_target_pairs={{0,1},{1,0},{2,3},{3,2},{4,5},{5,4},{6,7},{7,6},{8,9},{9,8},{10,11... | collective-permute-start | bytes 393224 | tf_op jit(solution)/shard_map/ppermute | solution.py:160
  54.3 1.0 %copy-start = (f32[256,256]{1,0:T(8,128)S(1)}, f32[256,256]{1,0:T(8,128)}, u32[]{:S(2)}) copy-start(f32[256,256]{1,0:T(8,128)} %get-tuple-element.8.p_ref) | copy-start | bytes 786436

commit v5 on v4

--- a/solution.py
+++ b/solution.py
@@ -65,12 +65,12 @@
         t = factor(b)
         states.append((mm(mm(t, b.astype(BF16)).astype(BF16), t, ABT), t.astype(F32) * jnp.sqrt(scale)))
     worst = jnp.sum(worst)
-    steps = jnp.int32(4)
-    for bound in (20.0, 45.0, 100.0, 180.0):
+    steps = jnp.int32(3)
+    for bound in (16.0, 24.0, 45.0, 100.0, 180.0):
         steps = steps + (worst > bound**4).astype(jnp.int32)
     extra = (worst > 48.0**4).astype(jnp.int32)
 
-    for growth in (1.3, 1.2, 1.0):
+    for growth in (1.3, 1.2):
         states = [step(b, x, growth) for b, x in states]
     for n, (b, x) in enumerate(states):
         b_ref[n] = b
@@ -87,7 +87,7 @@
             x_ref[n] = x_ref[n] - mm3(split(error(x, n)), x)
         return carry
 
-    lax.fori_loop(4, steps, more, 0)
+    lax.fori_loop(3, steps, more, 0)
     lax.fori_loop(0, extra, fix, 0)
     outs = []
     for n in range(len(problems)):
@@ -101,37 +101,38 @@
     return jnp.sum(jnp.sum(value, axis=1, keepdims=True), axis=0, keepdims=True)
 
 
-def leaf_kernel(s_ref, u_ref, out_ref, send_ref, *refs):
-    s, u = s_ref[...], u_ref[...]
+def leaf_kernel(rows_ref, out_ref, send_ref, *refs):
+    s, u = rows_ref[0], rows_ref[1]
     wide = s.astype(F32)
-    (out,) = whiten([(mm(s, s, ATB), total(wide * wide), mm(s, u, ATB))], *refs)
+    s_t = s.T
+    (out,) = whiten([(mm(s_t, s), total(wide * wide), mm(s_t, u))], *refs)
     out_ref[...] = out
     send_ref[...] = out.astype(BF16)
 
 
+def product(left, right):
+    out = mm(left[0], right[0])
+    if left[1] is not None:
+        out += mm(left[1], right[0])
+    if right[1] is not None:
+        out += mm(left[0], right[1])
+    return out
+
+
 def merge_parts(p, q):
-    gram, squares = 0.0, 0.0
+    p_t, q_t = (tuple(None if part is None else part.T for part in node) for node in (p, q))
+    squares = 0.0
     for high, low in (p, q):
-        if low is None:
-            wide = high.astype(F32)
-            gram += mm(high, high, ATB)
-        else:
-            wide = high.astype(F32) + low.astype(F32)
-            gram += mm3((high, low), (high, low), ATB)
+        wide = high.astype(F32) if low is None else high.astype(F32) + low.astype(F32)
         squares += total(wide * wide)
-    cross = mm(p[0], q[0], ATB)
-    if p[1] is not None:
-        cross += mm(p[1], q[0], ATB)
-    if q[1] is not None:
-        cross += mm(p[0], q[1], ATB)
-    return gram, squares, cross + cross.T
-
-
-def merge_kernel(p_ref, q1_ref, q2_ref, q3_ref, out_ref, *refs):
+    return product(p_t, p) + product(q_t, q), squares, product(p_t, q) + product(q_t, p)
+
+
+def merge_kernel(p_ref, q_ref, out_ref, *refs):
     near, far = whiten(
         [
-            merge_parts(split(p_ref[...]), (q1_ref[...], None)),
-            merge_parts((q2_ref[...], None), (q3_ref[...], None)),
+            merge_parts(split(p_ref[...]), (q_ref[0], None)),
+            merge_parts((q_ref[1], None), (q_ref[2], None)),
         ],
         *refs,
     )
@@ -139,7 +140,7 @@
 
 
 def dense_call(kernel, out_shapes, problems, *args):
-    width = args[0].shape[1]
+    width = args[0].shape[-1]
     whole = pl.BlockSpec(memory_space=pltpu.VMEM)
     return pl.pallas_call(
         kernel,
@@ -151,13 +152,42 @@
             pltpu.VMEM((problems, width, width), F32),
             pltpu.VMEM((problems, 2, width, width), BF16),
         ],
-        compiler_params=pltpu.CompilerParams(vmem_limit_bytes=16 * 2**20),
+        compiler_params=pltpu.CompilerParams(vmem_limit_bytes=67043328),
     )(*args)
 
 
-def from_partner(value, axis, mask):
-    pairs = [(source, source ^ mask) for source in range(lax.axis_size(axis))]
-    return lax.ppermute(value, axis, pairs)
+def gather_kernel(sent, out, send_sem, recv_sem):
+    j = lax.axis_index("col")
+    z = j % 4
+    peers = [j - z + near for near in (z + 1 - 2 * (z % 2), (z + 2) % 4, 3 - z)]
+    mesh_id = pl.DeviceIdType.MESH
+    barrier = pltpu.get_barrier_semaphore()
+    for peer in peers:
+        pl.semaphore_signal(barrier, inc=1, device_id={"col": peer}, device_id_type=mesh_id)
+    pl.semaphore_wait(barrier, 3)
+    copies = [
+        pltpu.make_async_remote_copy(
+            src_ref=sent, dst_ref=out.at[n], send_sem=send_sem.at[n], recv_sem=recv_sem.at[n],
+            device_id={"col": peer}, device_id_type=mesh_id,
+        )
+        for n, peer in enumerate(peers)
+    ]
+    for n in (1, 0, 2):
+        copies[n].start()
+    for copy in copies:
+        copy.wait()
+
+
+def gather_call(sent):
+    anywhere = pl.BlockSpec(memory_space=pl.ANY)
+    return pl.pallas_call(
+        gather_kernel,
+        out_shape=jax.ShapeDtypeStruct((3, *sent.shape), sent.dtype),
+        in_specs=[anywhere],
+        out_specs=anywhere,
+        scratch_shapes=[pltpu.SemaphoreType.DMA((3,)), pltpu.SemaphoreType.DMA((3,))],
+        compiler_params=pltpu.CompilerParams(collective_id=1, has_side_effects=True, vmem_limit_bytes=67043328),
+    )(sent)
 
 
 def iota(shape, axis):
@@ -186,9 +216,9 @@
 
 
 def sample_kernel(
-    rows_n, cols_n, a_hbm, right_hbm, left_hbm, leaf_hbm, tree_hbm, s_out, u_out,
+    rows_n, cols_n, a_hbm, right_hbm, left_hbm, leaf_hbm, tree_hbm, out,
     leaf_ref, tree_ref, a_buf, right_buf, left_buf, fs, fr, back, bs, bp, bsum, br,
-    f1s, f1r, f2s, f2r, b1s, b1r, b2s, b2r,
+    f1s, f1r, f2s, b1s, b1r, b2s, acc,
     in_sem, fs_sem, fr_sem, ps_sem, pr_sem, bs_sem, br_sem,
     f1s_sem, f1r_sem, f2s_sem, f2r_sem, b1s_sem, b1r_sem, b2s_sem, b2r_sem,
 ):
@@ -196,7 +226,8 @@
     lanes = fs.shape[1]
     group = cols_n // 4
     step_rows = group * lanes
-    y0 = j // group
+    y0, z0 = j // group, j % group
+    far_first = (2, 1, 3, 0)
     x0, core = i // 2, i % 2
     mesh_id = pl.DeviceIdType.MESH
 
@@ -224,32 +255,45 @@
     tree_copy = pltpu.make_async_copy(tree_hbm, tree_ref, in_sem.at[7])
 
     def rows_at(t):
-        return pl.ds(pl.multiple_of(((y0 + 1 + t) % 4) * step_rows, step_rows), step_rows)
+        return pl.ds(pl.multiple_of(((y0 + far_first[t]) % 4) * step_rows, step_rows), step_rows)
 
     def a_copy(t):
         return pltpu.make_async_copy(a_hbm.at[rows_at(t)], a_buf.at[rows_at(t)], in_sem.at[t])
 
     leaf_copy.start()
     tree_copy.start()
+    a_copy(0).start()
+    right_copy.start()
+    a_copy(1).start()
     left_copy.start()
-    for t in range(4):
-        a_copy(t).start()
-    right_copy.start()
+    a_copy(2).start()
+    a_copy(3).start()
     leaf_copy.wait()
     tree_copy.wait()
     tiles = a_buf.shape[1] // lanes
-    for t in range(4):
+    for t, dy in enumerate(far_first):
         a_copy(t).wait()
-        if t == 0:
-            left_copy.wait()
-        base = pl.multiple_of(((y0 + 1 + t) % 4) * step_rows, step_rows)
+        y = (y0 + dy) % 4
+        base = pl.multiple_of(y * step_rows, step_rows)
         for k in range(group):
-            mine = column_of(leaf_ref[pl.ds(i * cols_n + base // lanes + k, 1), :]).astype(BF16)
+            mine = column_of(leaf_ref[pl.ds(i * cols_n + y * group + k, 1), :]).astype(BF16)
             rows = pl.ds(pl.multiple_of(base + k * lanes, lanes), lanes)
             for c in range(tiles):
                 theirs = leaf_ref[pl.ds(j * rows_n + c, 1), :].astype(BF16)
                 block = a_buf[rows, c * lanes : (c + 1) * lanes]
                 a_buf[rows, c * lanes : (c + 1) * lanes] = jnp.where(mine == theirs, jnp.zeros_like(block), block)
+        if t == 0:
+            right_copy.wait()
+        forward = mm(a_buf[pl.ds(base, step_rows), :], right_buf[...]).astype(BF16)
+        fs[pl.ds(y * group, group)] = forward.reshape(group, lanes, forward.shape[1])
+        if t == 0:
+            pl.semaphore_wait(barrier, cols_n + rows_n - 2)
+        for dz in far_first:
+            if (dy, dz) != (0, 0):
+                peer = y * group + (z0 + dz) % group
+                remote(fs.at[peer], fr.at[j], fs_sem.at[peer], fr_sem.at[j], {"col": peer}).start()
+        if t == 0:
+            left_copy.wait()
         part = mm(left_buf[pl.ds(base, step_rows), :], a_buf[pl.ds(base, step_rows), :], ATB)
         if t == 0:
             back[...] = part
@@ -259,7 +303,6 @@
             part += back[...]
             for k in range(rows_n):
                 bs[k % 2, k // 2] = part[:, k * lanes : (k + 1) * lanes]
-    pl.semaphore_wait(barrier, cols_n + rows_n - 2)
     other = 1 - core
     chips = rows_n // 2
 
@@ -272,24 +315,6 @@
         return carry
 
     lax.fori_loop(0, chips, pair_start, 0)
-    right_copy.wait()
-
-    def compute(t, carry):
-        y = (y0 + 1 + t) % 4
-        base = pl.multiple_of(y * step_rows, step_rows)
-        forward = mm(a_buf[pl.ds(base, step_rows), :], right_buf[...]).astype(BF16)
-        fs[pl.ds(y * group, group)] = forward.reshape(group, lanes, forward.shape[1])
-        for k in range(group):
-            peer = y * group + (j + k) % group
-
-            @pl.when(peer != j)
-            def _():
-                remote(fs.at[peer], fr.at[j], fs_sem.at[peer], fr_sem.at[j], {"col": peer}).start()
-
-        return carry
-
-    lax.fori_loop(0, 4, compute, 0)
-    fr[pl.ds(j, 1)] = fs[pl.ds(j, 1)]
 
     def along(x):
         return remote(bsum.at[x], br.at[x0], bs_sem.at[x], br_sem.at[x0], {"row": x * 2 + core})
@@ -308,7 +333,7 @@
     lax.fori_loop(0, chips, pair_end, 0)
 
     tree = tree_ref[...]
-    slots = s_out.shape[0]
+    slots = out.shape[1]
     slot = iota((slots, lanes), 0)
     row_bits, col_bits = rows_n.bit_length() - 1, cols_n.bit_length() - 1
     f_place = (((slot >> 1) & (rows_n - 1)) << col_bits) + (slot >> (1 + row_bits))
@@ -324,7 +349,7 @@
     lax.fori_loop(0, chips - 1, along_end, 0)
     br[pl.ds(x0, 1)] = bsum[pl.ds(x0, 1)]
     sample_back = jnp.sum(br[...], axis=0).astype(BF16)
-    width = s_out.shape[1]
+    width = out.shape[2]
 
     def rows_exchange(src, dst, send_sem, recv_sem):
         def start(k, carry):
@@ -353,20 +378,48 @@
         return start, end
 
     b1_start, b1_end = rows_exchange(b1s, b1r, b1s_sem, b1r_sem)
-    b2_start, b2_end = cols_exchange(b2s, b2r, b2s_sem, b2r_sem)
     f1_start, f1_end = cols_exchange(f1s, f1r, f1s_sem, f1r_sem)
-    f2_start, f2_end = rows_exchange(f2s, f2r, f2s_sem, f2r_sem)
-    f0_end = cols_exchange(fs, fr, fs_sem, fr_sem)[1]
+
+    def back_part(col):
+        return out.at[1, pl.ds(pl.multiple_of(col * 2 * rows_n, 2 * rows_n), 2 * rows_n)]
+
+    def forward_part(row):
+        return out.at[0, pl.ds(pl.multiple_of(row * 2 * cols_n, 2 * cols_n), 2 * cols_n)]
+
+    def b2_start(k, carry):
+        peer = (j + k) % cols_n
+        remote(b2s.at[peer], back_part(j), b2s_sem.at[peer], b2r_sem.at[j], {"col": peer}).start()
+        return carry
+
+    def b2_end(k, carry):
+        peer = (j + k) % cols_n
+        remote(b2s.at[peer], back_part(peer), b2s_sem.at[peer], b2r_sem.at[peer], {"col": peer}).wait()
+        return carry
+
+    def f2_start(k, carry):
+        peer = (i + k) % rows_n
+        remote(f2s.at[peer], forward_part(i), f2s_sem.at[peer], f2r_sem.at[i], {"row": peer}).start()
+        return carry
+
+    def f2_end(k, carry):
+        peer = (i + k) % rows_n
+        remote(f2s.at[peer], forward_part(peer), f2s_sem.at[peer], f2r_sem.at[peer], {"row": peer}).wait()
+        return carry
 
     b1s[...] = mm(backward_map, sample_back, ABT).astype(BF16).reshape(b1s.shape)
     lax.fori_loop(1, rows_n, b1_start, 0)
     b1r[pl.ds(i, 1)] = b1s[pl.ds(i, 1)]
 
-    lax.fori_loop(1, cols_n, f0_end, 0)
-    forward_sum = fr[0].astype(F32)
-    for k in range(1, cols_n):
-        forward_sum += fr[k].astype(F32)
-    f1s[...] = mm(forward_map, forward_sum.astype(BF16)).astype(BF16).reshape(f1s.shape)
+    acc[...] = fs[pl.ds(j, 1)][0].astype(F32)
+    near_first = sorted(
+        ((dy, dz) for dy in range(4) for dz in range(4) if (dy, dz) != (0, 0)),
+        key=lambda d: min(d[0], 4 - d[0]) + min(d[1], 4 - d[1]),
+    )
+    for dy, dz in near_first:
+        peer = ((y0 + dy) % 4) * group + (z0 + dz) % group
+        remote(fs.at[peer], fr.at[peer], fs_sem.at[peer], fr_sem.at[peer], {"col": peer}).wait()
+        acc[...] += fr[pl.ds(peer, 1)][0].astype(F32)
+    f1s[...] = mm(forward_map, acc[...].astype(BF16)).astype(BF16).reshape(f1s.shape)
     lax.fori_loop(1, cols_n, f1_start, 0)
     f1r[pl.ds(j, 1)] = f1s[pl.ds(j, 1)]
 
@@ -379,17 +432,19 @@
     lax.fori_loop(1, rows_n, b1_end, 0)
     b2s[...] = mm(to_cols, b1r[...].reshape(slots, width)).astype(BF16).reshape(b2s.shape)
     lax.fori_loop(1, cols_n, b2_start, 0)
-    b2r[pl.ds(j, 1)] = b2s[pl.ds(j, 1)]
+    back_own = pltpu.make_async_copy(b2s.at[j], back_part(j), in_sem.at[4])
+    back_own.start()
 
     lax.fori_loop(1, cols_n, f1_end, 0)
     f2s[...] = mm(to_rows, f1r[...].reshape(slots, width)).astype(BF16).reshape(f2s.shape)
     lax.fori_loop(1, rows_n, f2_start, 0)
-    f2r[pl.ds(i, 1)] = f2s[pl.ds(i, 1)]
-
+    forward_own = pltpu.make_async_copy(f2s.at[i], forward_part(i), in_sem.at[5])
+    forward_own.start()
+
+    back_own.wait()
+    forward_own.wait()
     lax.fori_loop(1, cols_n, b2_end, 0)
-    u_out[...] = b2r[...].reshape(slots, width)
     lax.fori_loop(1, rows_n, f2_end, 0)
-    s_out[...] = f2r[...].reshape(slots, width)
 
 
 def sample_call(front_block, probe_right, probe_left, leaves, tree, rows_n, cols_n):
@@ -398,17 +453,16 @@
     lanes = leaves.shape[1]
     slots = 2 * rows_n * cols_n
     chips = rows_n // 2
-    vmem = pl.BlockSpec(memory_space=pltpu.VMEM)
     hbm = pl.BlockSpec(memory_space=pltpu.HBM)
-    out = jax.ShapeDtypeStruct((slots, samples), BF16)
+    out = jax.ShapeDtypeStruct((2, slots, samples), BF16)
     by_col = pltpu.VMEM((cols_n, 2 * rows_n, samples), BF16)
     by_row = pltpu.VMEM((rows_n, 2 * cols_n, samples), BF16)
     dma = pltpu.SemaphoreType.DMA
     return pl.pallas_call(
         functools.partial(sample_kernel, rows_n, cols_n),
-        out_shape=(out, out),
+        out_shape=out,
         in_specs=[hbm] * 5,
-        out_specs=(vmem, vmem),
+        out_specs=pl.BlockSpec(memory_space=pl.ANY),
         scratch_shapes=[
             pltpu.VMEM(leaves.shape, jnp.int32),
             pltpu.VMEM(tree.shape, jnp.int32),
@@ -422,7 +476,8 @@
             pltpu.VMEM((chips, samples, lanes), F32),
             pltpu.VMEM((chips, samples, lanes), F32),
             pltpu.VMEM((chips, samples, lanes), F32),
-            by_col, by_col, by_row, by_row, by_row, by_row, by_col, by_col,
+            by_col, by_col, by_row, by_row, by_row, by_col,
+            pltpu.VMEM((lanes, samples), F32),
             dma((8,)),
             dma((cols_n,)), dma((cols_n,)),
             dma((chips,)), dma((chips,)), dma((chips,)), dma((chips,)),
@@ -437,12 +492,9 @@
     rows_n, cols_n = lax.axis_size("row"), lax.axis_size("col")
     devices = rows_n * cols_n
     leaves = row_leaf.reshape(devices, row_leaf.shape[0] // devices)
-    forward_recv, backward_recv = sample_call(
-        front_block, probe_right, probe_left, leaves, tree_leaf.reshape(1, devices), rows_n, cols_n
-    )
-    coupling, sent = dense_call(leaf_kernel, (F32, BF16), 1, forward_recv, backward_recv)
-    others = [from_partner(sent, "col", mask) for mask in (1, 2, 3)]
-    (merged,) = dense_call(merge_kernel, (F32,), 2, coupling, *others)
+    routed = sample_call(front_block, probe_right, probe_left, leaves, tree_leaf.reshape(1, devices), rows_n, cols_n)
+    coupling, sent = dense_call(leaf_kernel, (F32, BF16), 1, routed)
+    (merged,) = dense_call(merge_kernel, (F32,), 2, coupling, gather_call(sent))
     return (coupling[None], merged[None])
 
 

time: 64 us -> 59.8 us (0.934)
  Pallas kernels: 51.2 us -> 58.9 us
  waiting for transfers between devices: 5.8 us -> 0 us
  starting transfers between devices: 3.25 us -> 0 us
  local copies, waits for them, and re-layouts: 2.75 us -> 0 us
    pallas_call x0 -> x1, Pallas kernels: none -> 9.71 us  [gather_call(): pl.pallas_call(gather_kernel, out_shape=jax.ShapeDtypeStruct((3, *sent.sh...]
    ppermute x3 -> x0, waiting for transfers between devices: 5.8 us -> none  [from_partner(): return lax.ppermute(value, axis, pairs)]
    pallas_call x1, Pallas kernels: 39.1 us -> 35.6 us  [sample_call(): pl.pallas_call(functools.partial(sample_kernel, rows_n, cols_n), out_shap...]
    ppermute x3 -> x0, starting transfers between devices: 3.25 us -> none  [from_partner(): return lax.ppermute(value, axis, pairs)]
    unnamed x6 -> x0, local copies, waits for them, and re-layouts: 2.75 us -> none
    pallas_call x2, Pallas kernels: 12.2 us -> 13.7 us  [dense_call(): pl.pallas_call(kernel, out_shape=tuple((jax.ShapeDtypeStruct((width, widt...]
  transfers between devices with their start and end apart: 3 -> 0, of which waited for: 3 -> 0; matrix products, arithmetic and copies ran while one was open for 0% -> 0% of each run, Pallas kernels for 0% -> 0%
where the time goes in v5:
time: 59.8 us; the launch traced here: 59.6 us
  Pallas kernels  58.9 us (98%)
  between operations  0.65 us (1%)
    pallas_call x1, Pallas kernels, sample_call(): pl.pallas_call(functools.partial(sample_kernel, rows_n, cols_n), out_shap...  35.6 us
    pallas_call x2, Pallas kernels, dense_call(): pl.pallas_call(kernel, out_shape=tuple((jax.ShapeDtypeStruct((width, widt...  13.7 us
    pallas_call x1, Pallas kernels, gather_call(): pl.pallas_call(gather_kernel, out_shape=jax.ShapeDtypeStruct((3, *sent.sh...  9.71 us

profile of v5, /device:TPU:1, one launch (start us, length us, event | category | flops | bytes accessed | tf_op | source)
XLA Modules:
  0.0 59.6 jit_solution(3065130894547183366)
XLA Ops:
  0.6 35.6 %shard_map.68.rows_ref = bf16[2,256,256]{2,1,0:T(8,128)(2,1)} custom-call(bf16[2048,1024]{1,0:T(8,128)(2,1)} %a_hbm.1, bf16[1024,256]{1,0:T(8,128)(2,1)} %right_hbm.1, bf16[2048,256]{1,0:T(8,128)(2,1)} %left_hbm.1, s32[128,128]{1,0:T(8,128)} %bitcast.6, s32[1,128]{1,0:T(1,128)} %bitcast.7), custom_call_target="tpu_custom_call" | custom-call | tf_op jit(solution)/shard_map/pallas_call | solution.py:461
  36.2 4.7 %shard_map.69 = (f32[256,256]{1,0:T(8,128)}, bf16[256,256]{1,0:T(8,128)(2,1)}) custom-call(bf16[2,256,256]{2,1,0:T(8,128)(2,1)} %shard_map.68.rows_ref), custom_call_target="tpu_custom_call" | custom-call | tf_op jit(solution)/shard_map/pallas_call | solution.py:145
  40.9 9.7 %shard_map.70.q_ref = bf16[3,256,256]{2,1,0:T(8,128)(2,1)} custom-call(bf16[256,256]{1,0:T(8,128)(2,1)} %get-tuple-element.5.sent), custom_call_target="tpu_custom_call" | custom-call | tf_op jit(solution)/shard_map/pallas_call | solution.py:183
  50.6 9.0 %shard_map.71 = f32[256,256]{1,0:T(8,128)} custom-call(f32[256,256]{1,0:T(8,128)} %get-tuple-element.4.p_ref, bf16[3,256,256]{2,1,0:T(8,128)(2,1)} %shard_map.70.q_ref), custom_call_target="tpu_custom_call" | custom-call | tf_op jit(solution)/shard_map/pallas_call | solution.py:145

commit v6 on v5

--- a/solution.py
+++ b/solution.py
@@ -39,15 +39,13 @@
     def factor(value):
         return jnp.where(below, -value, jnp.where(diag, 1.5 - 0.5 * value, 0.0)).astype(BF16)
 
-    def step(b, x, growth):
-        b = b * growth
-        t = factor(b)
-        y = mm(t, b.astype(BF16))
-        return mm(y.astype(BF16), t, ABT), mm(t, (x * growth**0.5).astype(BF16))
+    def advance(b, t, growth):
+        b = mm(mm(t, b.astype(BF16)).astype(BF16), t, ABT) * growth
+        return b, factor(b)
 
     def error(x, n):
-        y = split(mm3(x, (g_ref[n, 0], g_ref[n, 1])))
-        return half(mm3(y, x, ABT) - diag.astype(F32))
+        y_high, y_low = split(mm(x, g_ref[n, 0]) + mm(x, g_ref[n, 1]))
+        return half(mm(y_high, x, ABT) + mm(y_low, x, ABT) - diag.astype(F32))
 
     rhs, worst, states = [], None, []
     for n, (gram, squares, cross) in enumerate(problems):
@@ -63,7 +61,7 @@
         scale = 1.9 * lax.rsqrt(jnp.sqrt(fourth))
         b = unit * scale
         t = factor(b)
-        states.append((mm(mm(t, b.astype(BF16)).astype(BF16), t, ABT), t.astype(F32) * jnp.sqrt(scale)))
+        states.append((b, t, t.astype(F32) * jnp.sqrt(scale * (1.3 * 1.2))))
     worst = jnp.sum(worst)
     steps = jnp.int32(3)
     for bound in (16.0, 24.0, 45.0, 100.0, 180.0):
@@ -71,28 +69,30 @@
     extra = (worst > 48.0**4).astype(jnp.int32)
 
     for growth in (1.3, 1.2):
-        states = [step(b, x, growth) for b, x in states]
-    for n, (b, x) in enumerate(states):
+        states = [(*advance(b, t, growth), x) for b, t, x in states]
+        states = [(b, t, mm(t, x.astype(BF16))) for b, t, x in states]
+    for n, (b, t, x) in enumerate(states):
         b_ref[n] = b
         x_ref[n] = x
 
     def more(_, carry):
         for n in range(len(problems)):
-            b_ref[n], x_ref[n] = step(b_ref[n], x_ref[n], 1.0)
+            b, t = advance(b_ref[n], factor(b_ref[n]), 1.0)
+            b_ref[n], x_ref[n] = b, mm(t, x_ref[n].astype(BF16))
         return carry
 
     def fix(_, carry):
         for n in range(len(problems)):
-            x = split(x_ref[n])
-            x_ref[n] = x_ref[n] - mm3(split(error(x, n)), x)
+            x = x_ref[n].astype(BF16)
+            x_ref[n] = x.astype(F32) - mm(error(x, n).astype(BF16), x)
         return carry
 
     lax.fori_loop(3, steps, more, 0)
     lax.fori_loop(0, extra, fix, 0)
     outs = []
     for n in range(len(problems)):
-        x = split(x_ref[n])
-        z = mm3(x, rhs[n])
+        x = x_ref[n].astype(BF16)
+        z = mm(x, rhs[n][0]) + mm(x, rhs[n][1])
         outs.append(z - mm(error(x, n).astype(BF16), z.astype(BF16)))
     return outs
 
@@ -130,11 +130,7 @@
 
 def merge_kernel(p_ref, q_ref, out_ref, *refs):
     near, far = whiten(
-        [
-            merge_parts(split(p_ref[...]), (q_ref[0], None)),
-            merge_parts((q_ref[1], None), (q_ref[2], None)),
-        ],
-        *refs,
+        [merge_parts((p_ref[...], None), (q_ref[0], None)), merge_parts((q_ref[1], None), (q_ref[2], None))], *refs
     )
     (out_ref[...],) = whiten([merge_parts(split(near), split(far))], *refs)
 
@@ -494,7 +490,7 @@
     leaves = row_leaf.reshape(devices, row_leaf.shape[0] // devices)
     routed = sample_call(front_block, probe_right, probe_left, leaves, tree_leaf.reshape(1, devices), rows_n, cols_n)
     coupling, sent = dense_call(leaf_kernel, (F32, BF16), 1, routed)
-    (merged,) = dense_call(merge_kernel, (F32,), 2, coupling, gather_call(sent))
+    (merged,) = dense_call(merge_kernel, (F32,), 2, sent, gather_call(sent))
     return (coupling[None], merged[None])
 
 

time: 59.8 us -> 59.8 us (level)
  no operation moved by 1% of the time
where the time goes in v6:
time: 59.8 us; the launch traced here: 59.4 us
  Pallas kernels  58.8 us (98%)
  between operations  0.65 us (1%)
    pallas_call x1, Pallas kernels, sample_call(): pl.pallas_call(functools.partial(sample_kernel, rows_n, cols_n), out_shap...  35.6 us
    pallas_call x2, Pallas kernels, dense_call(): pl.pallas_call(kernel, out_shape=tuple((jax.ShapeDtypeStruct((width, widt...  13.5 us
    pallas_call x1, Pallas kernels, gather_call(): pl.pallas_call(gather_kernel, out_shape=jax.ShapeDtypeStruct((3, *sent.sh...  9.65 us

profile of v6, /device:TPU:1, one launch (start us, length us, event | category | flops | bytes accessed | tf_op | source)
XLA Modules:
  0.0 59.4 jit_solution(16110711886630373819)
XLA Ops:
  0.6 35.6 %shard_map.68.rows_ref = bf16[2,256,256]{2,1,0:T(8,128)(2,1)} custom-call(bf16[2048,1024]{1,0:T(8,128)(2,1)} %a_hbm.1, bf16[1024,256]{1,0:T(8,128)(2,1)} %right_hbm.1, bf16[2048,256]{1,0:T(8,128)(2,1)} %left_hbm.1, s32[128,128]{1,0:T(8,128)} %bitcast.5, s32[1,128]{1,0:T(1,128)} %bitcast.6), custom_call_target="tpu_custom_call" | custom-call | tf_op jit(solution)/shard_map/pallas_call | solution.py:457
  36.2 4.6 %shard_map.69 = (f32[256,256]{1,0:T(8,128)}, bf16[256,256]{1,0:T(8,128)(2,1)}) custom-call(bf16[2,256,256]{2,1,0:T(8,128)(2,1)} %shard_map.68.rows_ref), custom_call_target="tpu_custom_call" | custom-call | tf_op jit(solution)/shard_map/pallas_call | solution.py:141
  40.8 9.7 %shard_map.70.q_ref = bf16[3,256,256]{2,1,0:T(8,128)(2,1)} custom-call(bf16[256,256]{1,0:T(8,128)(2,1)} %get-tuple-element.5.sent.p_ref), custom_call_target="tpu_custom_call" | custom-call | tf_op jit(solution)/shard_map/pallas_call | solution.py:179
  50.4 9.0 %shard_map.71 = f32[256,256]{1,0:T(8,128)} custom-call(bf16[256,256]{1,0:T(8,128)(2,1)} %get-tuple-element.5.sent.p_ref, bf16[3,256,256]{2,1,0:T(8,128)(2,1)} %shard_map.70.q_ref), custom_call_target="tpu_custom_call" | custom-call | tf_op jit(solution)/shard_map/pallas_call | solution.py:141

commit v7 on v6

--- a/solution.py
+++ b/solution.py
@@ -213,7 +213,7 @@
 
 def sample_kernel(
     rows_n, cols_n, a_hbm, right_hbm, left_hbm, leaf_hbm, tree_hbm, out,
-    leaf_ref, tree_ref, a_buf, right_buf, left_buf, fs, fr, back, bs, bp, bsum, br,
+    leaf_ref, tree_ref, a_buf, right_buf, left_buf, left_t, fs, fr, bs, bp, bsum, br,
     f1s, f1r, f2s, b1s, b1r, b2s, acc,
     in_sem, fs_sem, fr_sem, ps_sem, pr_sem, bs_sem, br_sem,
     f1s_sem, f1r_sem, f2s_sem, f2r_sem, b1s_sem, b1r_sem, b2s_sem, b2r_sem,
@@ -246,7 +246,6 @@
     lax.fori_loop(1, rows_n, greet_row, 0)
 
     right_copy = pltpu.make_async_copy(right_hbm, right_buf, in_sem.at[4])
-    left_copy = pltpu.make_async_copy(left_hbm, left_buf, in_sem.at[5])
     leaf_copy = pltpu.make_async_copy(leaf_hbm, leaf_ref, in_sem.at[6])
     tree_copy = pltpu.make_async_copy(tree_hbm, tree_ref, in_sem.at[7])
 
@@ -254,79 +253,96 @@
         return pl.ds(pl.multiple_of(((y0 + far_first[t]) % 4) * step_rows, step_rows), step_rows)
 
     def a_copy(t):
-        return pltpu.make_async_copy(a_hbm.at[rows_at(t)], a_buf.at[rows_at(t)], in_sem.at[t])
+        return pltpu.make_async_copy(a_hbm.at[rows_at(t)], a_buf.at[pl.ds(t * step_rows, step_rows)], in_sem.at[t])
+
+    def left_copy(t):
+        return pltpu.make_async_copy(
+            left_hbm.at[rows_at(t)], left_buf.at[pl.ds(t * step_rows, step_rows)], in_sem.at[8 + t]
+        )
 
     leaf_copy.start()
     tree_copy.start()
     a_copy(0).start()
     right_copy.start()
-    a_copy(1).start()
-    left_copy.start()
-    a_copy(2).start()
-    a_copy(3).start()
-    leaf_copy.wait()
-    tree_copy.wait()
+    for t in range(1, 4):
+        a_copy(t).start()
+    for t in range(4):
+        left_copy(t).start()
     tiles = a_buf.shape[1] // lanes
-    for t, dy in enumerate(far_first):
-        a_copy(t).wait()
-        y = (y0 + dy) % 4
-        base = pl.multiple_of(y * step_rows, step_rows)
+
+    def mask(t):
+        y = (y0 + far_first[t]) % 4
         for k in range(group):
             mine = column_of(leaf_ref[pl.ds(i * cols_n + y * group + k, 1), :]).astype(BF16)
-            rows = pl.ds(pl.multiple_of(base + k * lanes, lanes), lanes)
+            rows = slice(t * step_rows + k * lanes, t * step_rows + (k + 1) * lanes)
             for c in range(tiles):
                 theirs = leaf_ref[pl.ds(j * rows_n + c, 1), :].astype(BF16)
                 block = a_buf[rows, c * lanes : (c + 1) * lanes]
                 a_buf[rows, c * lanes : (c + 1) * lanes] = jnp.where(mine == theirs, jnp.zeros_like(block), block)
-        if t == 0:
-            right_copy.wait()
-        forward = mm(a_buf[pl.ds(base, step_rows), :], right_buf[...]).astype(BF16)
-        fs[pl.ds(y * group, group)] = forward.reshape(group, lanes, forward.shape[1])
-        if t == 0:
-            pl.semaphore_wait(barrier, cols_n + rows_n - 2)
-        for dz in far_first:
-            if (dy, dz) != (0, 0):
-                peer = y * group + (z0 + dz) % group
-                remote(fs.at[peer], fr.at[j], fs_sem.at[peer], fr_sem.at[j], {"col": peer}).start()
-        if t == 0:
-            left_copy.wait()
-        part = mm(left_buf[pl.ds(base, step_rows), :], a_buf[pl.ds(base, step_rows), :], ATB)
-        if t == 0:
-            back[...] = part
-        elif t < 3:
-            back[...] += part
-        else:
-            part += back[...]
-            for k in range(rows_n):
-                bs[k % 2, k // 2] = part[:, k * lanes : (k + 1) * lanes]
+
+    def forward(t):
+        y = (y0 + far_first[t]) % 4
+        part = mm(a_buf[t * step_rows : (t + 1) * step_rows, :], right_buf[...]).astype(BF16)
+        fs[pl.ds(y * group, group)] = part.reshape(group, lanes, part.shape[1])
+
+    def turn(t):
+        rows = slice(t * step_rows, (t + 1) * step_rows)
+        left_t[:, rows] = left_buf[rows, :].T
+
+    def distance(d):
+        return min(d[0], 4 - d[0]) + min(d[1], 4 - d[1])
+
+    near_first = sorted(((dy, dz) for dy in range(4) for dz in range(4) if (dy, dz) != (0, 0)), key=distance)
+
+    leaf_copy.wait()
+    tree_copy.wait()
+    a_copy(0).wait()
+    mask(0)
+    right_copy.wait()
+    a_copy(1).wait()
+    mask(1)
+    forward(0)
+    a_copy(2).wait()
+    left_copy(0).wait()
+    left_copy(1).wait()
+    mask(2)
+    forward(1)
+    turn(0)
+    turn(1)
+    a_copy(3).wait()
+    left_copy(2).wait()
+    left_copy(3).wait()
+    mask(3)
+    forward(2)
+    turn(2)
+    turn(3)
+    forward(3)
+    pl.semaphore_wait(barrier, cols_n + rows_n - 2)
+    for dy, dz in reversed(near_first):
+        peer = ((y0 + dy) % 4) * group + (z0 + dz) % group
+        remote(fs.at[peer], fr.at[j], fs_sem.at[peer], fr_sem.at[j], {"col": peer}).start()
+
     other = 1 - core
     chips = rows_n // 2
 
-    def pair(k):
-        x = (x0 + 1 + k) % chips
-        return x, remote(bs.at[other, x], bp.at[x], ps_sem.at[x], pr_sem.at[x], {"row": x0 * 2 + other})
-
-    def pair_start(k, carry):
-        pair(k)[1].start()
-        return carry
-
-    lax.fori_loop(0, chips, pair_start, 0)
+    def pair(x):
+        return remote(bs.at[other, x], bp.at[x], ps_sem.at[x], pr_sem.at[x], {"row": x0 * 2 + other})
 
     def along(x):
         return remote(bsum.at[x], br.at[x0], bs_sem.at[x], br_sem.at[x0], {"row": x * 2 + core})
 
-    def pair_end(k, carry):
-        x, copy = pair(k)
-        copy.wait()
+    for dx in far_first:
+        x = (x0 + dx) % chips
+        part = mm(left_t[...], a_buf[:, pl.ds(pl.multiple_of(x * 2 * lanes, 2 * lanes), 2 * lanes)])
+        bs[0, pl.ds(x, 1)] = part[None, :, :lanes]
+        bs[1, pl.ds(x, 1)] = part[None, :, lanes:]
+        pair(x).start()
+    for dx in far_first:
+        x = (x0 + dx) % chips
+        pair(x).wait()
         bsum[pl.ds(x, 1)] = bs[core, pl.ds(x, 1)] + bp[pl.ds(x, 1)]
-
-        @pl.when(x != x0)
-        def _():
+        if dx:
             along(x).start()
-
-        return carry
-
-    lax.fori_loop(0, chips, pair_end, 0)
 
     tree = tree_ref[...]
     slots = out.shape[1]
@@ -407,10 +423,6 @@
     b1r[pl.ds(i, 1)] = b1s[pl.ds(i, 1)]
 
     acc[...] = fs[pl.ds(j, 1)][0].astype(F32)
-    near_first = sorted(
-        ((dy, dz) for dy in range(4) for dz in range(4) if (dy, dz) != (0, 0)),
-        key=lambda d: min(d[0], 4 - d[0]) + min(d[1], 4 - d[1]),
-    )
     for dy, dz in near_first:
         peer = ((y0 + dy) % 4) * group + (z0 + dz) % group
         remote(fs.at[peer], fr.at[peer], fs_sem.at[peer], fr_sem.at[peer], {"col": peer}).wait()
@@ -465,16 +477,16 @@
             pltpu.VMEM((tile_rows, tile_cols), BF16),
             pltpu.VMEM((tile_cols, samples), BF16),
             pltpu.VMEM((tile_rows, samples), BF16),
+            pltpu.VMEM((samples, tile_rows), BF16),
             pltpu.VMEM((cols_n, lanes, samples), BF16),
             pltpu.VMEM((cols_n, lanes, samples), BF16),
-            pltpu.VMEM((samples, tile_cols), F32),
             pltpu.VMEM((2, chips, samples, lanes), F32),
             pltpu.VMEM((chips, samples, lanes), F32),
             pltpu.VMEM((chips, samples, lanes), F32),
             pltpu.VMEM((chips, samples, lanes), F32),
             by_col, by_col, by_row, by_row, by_row, by_col,
             pltpu.VMEM((lanes, samples), F32),
-            dma((8,)),
+            dma((12,)),
             dma((cols_n,)), dma((cols_n,)),
             dma((chips,)), dma((chips,)), dma((chips,)), dma((chips,)),
             dma((cols_n,)), dma((cols_n,)), dma((rows_n,)), dma((rows_n,)),

time: 59.8 us -> 58.8 us (0.983)
  Pallas kernels: 58.8 us -> 57.4 us
    pallas_call x2, Pallas kernels: 13.5 us -> 12.3 us  [dense_call(): pl.pallas_call(kernel, out_shape=tuple((jax.ShapeDtypeStruct((width, widt...]
where the time goes in v7:
time: 58.8 us; the launch traced here: 58.1 us
  Pallas kernels  57.4 us (98%)
  between operations  0.65 us (1%)
    pallas_call x1, Pallas kernels, sample_call(): pl.pallas_call(functools.partial(sample_kernel, rows_n, cols_n), out_shap...  35.2 us
    pallas_call x2, Pallas kernels, dense_call(): pl.pallas_call(kernel, out_shape=tuple((jax.ShapeDtypeStruct((width, widt...  12.3 us
    pallas_call x1, Pallas kernels, gather_call(): pl.pallas_call(gather_kernel, out_shape=jax.ShapeDtypeStruct((3, *sent.sh...  9.95 us

profile of v7, /device:TPU:1, one launch (start us, length us, event | category | flops | bytes accessed | tf_op | source)
XLA Modules:
  0.0 58.1 jit_solution(4778242241891225742)
XLA Ops:
  0.6 35.2 %shard_map.68.rows_ref = bf16[2,256,256]{2,1,0:T(8,128)(2,1)} custom-call(bf16[2048,1024]{1,0:T(8,128)(2,1)} %a_hbm.1, bf16[1024,256]{1,0:T(8,128)(2,1)} %right_hbm.1, bf16[2048,256]{1,0:T(8,128)(2,1)} %left_hbm.1, s32[128,128]{1,0:T(8,128)} %bitcast.5, s32[1,128]{1,0:T(1,128)} %bitcast.6), custom_call_target="tpu_custom_call" | custom-call | tf_op jit(solution)/shard_map/pallas_call | solution.py:469
  35.9 4.1 %shard_map.69 = (f32[256,256]{1,0:T(8,128)}, bf16[256,256]{1,0:T(8,128)(2,1)}) custom-call(bf16[2,256,256]{2,1,0:T(8,128)(2,1)} %shard_map.68.rows_ref), custom_call_target="tpu_custom_call" | custom-call | tf_op jit(solution)/shard_map/pallas_call | solution.py:141
  40.0 9.9 %shard_map.70.q_ref = bf16[3,256,256]{2,1,0:T(8,128)(2,1)} custom-call(bf16[256,256]{1,0:T(8,128)(2,1)} %get-tuple-element.5.sent.p_ref), custom_call_target="tpu_custom_call" | custom-call | tf_op jit(solution)/shard_map/pallas_call | solution.py:179
  49.9 8.2 %shard_map.71 = f32[256,256]{1,0:T(8,128)} custom-call(bf16[256,256]{1,0:T(8,128)(2,1)} %get-tuple-element.5.sent.p_ref, bf16[3,256,256]{2,1,0:T(8,128)(2,1)} %shard_map.70.q_ref), custom_call_target="tpu_custom_call" | custom-call | tf_op jit(solution)/shard_map/pallas_call | solution.py:141

commit v8 on v7

--- a/solution.py
+++ b/solution.py
@@ -125,7 +125,7 @@
     for high, low in (p, q):
         wide = high.astype(F32) if low is None else high.astype(F32) + low.astype(F32)
         squares += total(wide * wide)
-    return product(p_t, p) + product(q_t, q), squares, product(p_t, q) + product(q_t, p)
+    return mm(p_t[0], p[0]) + mm(q_t[0], q[0]), squares, product(p_t, q) + product(q_t, p)
 
 
 def merge_kernel(p_ref, q_ref, out_ref, *refs):
@@ -148,7 +148,7 @@
             pltpu.VMEM((problems, width, width), F32),
             pltpu.VMEM((problems, 2, width, width), BF16),
         ],
-        compiler_params=pltpu.CompilerParams(vmem_limit_bytes=67043328),
+        compiler_params=pltpu.CompilerParams(vmem_limit_bytes=16 * 2**20),
     )(*args)
 
 
@@ -182,7 +182,7 @@
         in_specs=[anywhere],
         out_specs=anywhere,
         scratch_shapes=[pltpu.SemaphoreType.DMA((3,)), pltpu.SemaphoreType.DMA((3,))],
-        compiler_params=pltpu.CompilerParams(collective_id=1, has_side_effects=True, vmem_limit_bytes=67043328),
+        compiler_params=pltpu.CompilerParams(collective_id=1, has_side_effects=True, vmem_limit_bytes=16 * 2**20),
     )(sent)
 
 
@@ -285,6 +285,12 @@
         part = mm(a_buf[t * step_rows : (t + 1) * step_rows, :], right_buf[...]).astype(BF16)
         fs[pl.ds(y * group, group)] = part.reshape(group, lanes, part.shape[1])
 
+    def send(t):
+        for dz in far_first:
+            if (far_first[t], dz) != (0, 0):
+                peer = ((y0 + far_first[t]) % 4) * group + (z0 + dz) % group
+                remote(fs.at[peer], fr.at[j], fs_sem.at[peer], fr_sem.at[j], {"col": peer}).start()
+
     def turn(t):
         rows = slice(t * step_rows, (t + 1) * step_rows)
         left_t[:, rows] = left_buf[rows, :].T
@@ -302,11 +308,14 @@
     a_copy(1).wait()
     mask(1)
     forward(0)
+    pl.semaphore_wait(barrier, cols_n + rows_n - 2)
+    send(0)
     a_copy(2).wait()
     left_copy(0).wait()
     left_copy(1).wait()
     mask(2)
     forward(1)
+    send(1)
     turn(0)
     turn(1)
     a_copy(3).wait()
@@ -314,13 +323,11 @@
     left_copy(3).wait()
     mask(3)
     forward(2)
+    send(2)
     turn(2)
     turn(3)
     forward(3)
-    pl.semaphore_wait(barrier, cols_n + rows_n - 2)
-    for dy, dz in reversed(near_first):
-        peer = ((y0 + dy) % 4) * group + (z0 + dz) % group
-        remote(fs.at[peer], fr.at[j], fs_sem.at[peer], fr_sem.at[j], {"col": peer}).start()
+    send(3)
 
     other = 1 - core
     chips = rows_n // 2
@@ -390,18 +397,13 @@
         return start, end
 
     b1_start, b1_end = rows_exchange(b1s, b1r, b1s_sem, b1r_sem)
-    f1_start, f1_end = cols_exchange(f1s, f1r, f1s_sem, f1r_sem)
+    f1_end = cols_exchange(f1s, f1r, f1s_sem, f1r_sem)[1]
 
     def back_part(col):
         return out.at[1, pl.ds(pl.multiple_of(col * 2 * rows_n, 2 * rows_n), 2 * rows_n)]
 
     def forward_part(row):
         return out.at[0, pl.ds(pl.multiple_of(row * 2 * cols_n, 2 * cols_n), 2 * cols_n)]
-
-    def b2_start(k, carry):
-        peer = (j + k) % cols_n
-        remote(b2s.at[peer], back_part(j), b2s_sem.at[peer], b2r_sem.at[j], {"col": peer}).start()
-        return carry
 
     def b2_end(k, carry):
         peer = (j + k) % cols_n
@@ -428,7 +430,9 @@
         remote(fs.at[peer], fr.at[peer], fs_sem.at[peer], fr_sem.at[peer], {"col": peer}).wait()
         acc[...] += fr[pl.ds(peer, 1)][0].astype(F32)
     f1s[...] = mm(forward_map, acc[...].astype(BF16)).astype(BF16).reshape(f1s.shape)
-    lax.fori_loop(1, cols_n, f1_start, 0)
+    for dy, dz in reversed(near_first):
+        peer = ((y0 + dy) % 4) * group + (z0 + dz) % group
+        remote(f1s.at[peer], f1r.at[j], f1s_sem.at[peer], f1r_sem.at[j], {"col": peer}).start()
     f1r[pl.ds(j, 1)] = f1s[pl.ds(j, 1)]
 
     slot = iota((slots, slots), 0)
@@ -439,7 +443,9 @@
 
     lax.fori_loop(1, rows_n, b1_end, 0)
     b2s[...] = mm(to_cols, b1r[...].reshape(slots, width)).astype(BF16).reshape(b2s.shape)
-    lax.fori_loop(1, cols_n, b2_start, 0)
+    for dy, dz in reversed(near_first):
+        peer = ((y0 + dy) % 4) * group + (z0 + dz) % group
+        remote(b2s.at[peer], back_part(j), b2s_sem.at[peer], b2r_sem.at[j], {"col": peer}).start()
     back_own = pltpu.make_async_copy(b2s.at[j], back_part(j), in_sem.at[4])
     back_own.start()
 

time: 58.8 us -> 57.1 us (0.971)
  Pallas kernels: 57.4 us -> 55.3 us
  local copies, waits for them, and re-layouts: 0 us -> 0.94 us
    unnamed x0 -> x2, local copies, waits for them, and re-layouts: none -> 0.94 us
    pallas_call x2, Pallas kernels: 12.3 us -> 11.4 us  [dense_call(): pl.pallas_call(kernel, out_shape=tuple((jax.ShapeDtypeStruct((width, widt...]
    pallas_call x1, Pallas kernels: 9.95 us -> 9.2 us  [gather_call(): pl.pallas_call(gather_kernel, out_shape=jax.ShapeDtypeStruct((3, *sent.sh...]
where the time goes in v8:
time: 57.1 us; the launch traced here: 56.9 us
  Pallas kernels  55.3 us (97%)
  local copies, waits for them, and re-layouts  0.94 us (2%)
  between operations  0.66 us (1%)
    pallas_call x1, Pallas kernels, sample_call(): pl.pallas_call(functools.partial(sample_kernel, rows_n, cols_n), out_shap...  34.7 us
    pallas_call x2, Pallas kernels, dense_call(): pl.pallas_call(kernel, out_shape=tuple((jax.ShapeDtypeStruct((width, widt...  11.4 us
    pallas_call x1, Pallas kernels, gather_call(): pl.pallas_call(gather_kernel, out_shape=jax.ShapeDtypeStruct((3, *sent.sh...  9.2 us

profile of v8, /device:TPU:1, one launch (start us, length us, event | category | flops | bytes accessed | tf_op | source)
XLA Modules:
  0.0 56.9 jit_solution(9695116463787415702)
XLA Ops:
  0.6 34.7 %shard_map.68.rows_ref = bf16[2,256,256]{2,1,0:T(8,128)(2,1)} custom-call(bf16[2048,1024]{1,0:T(8,128)(2,1)} %a_hbm.1, bf16[1024,256]{1,0:T(8,128)(2,1)} %right_hbm.1, bf16[2048,256]{1,0:T(8,128)(2,1)} %left_hbm.1, s32[128,128]{1,0:T(8,128)} %bitcast.5, s32[1,128]{1,0:T(1,128)} %bitcast.6), custom_call_target="tpu_custom_call" | custom-call | tf_op jit(solution)/shard_map/pallas_call | solution.py:475
  35.4 0.0 copy-start
  35.4 0.9 %copy-done = bf16[2,256,256]{2,1,0:T(8,128)(2,1)S(1)} copy-done((bf16[2,256,256]{2,1,0:T(8,128)(2,1)S(1)}, bf16[2,256,256]{2,1,0:T(8,128)(2,1)}, u32[]{:S(2)}) %copy-start) | copy-done | bytes 262168
  36.3 3.6 %shard_map.69 = (f32[256,256]{1,0:T(8,128)}, bf16[256,256]{1,0:T(8,128)(2,1)S(1)}) custom-call(bf16[2,256,256]{2,1,0:T(8,128)(2,1)S(1)} %copy-done), custom_call_target="tpu_custom_call" | custom-call | tf_op jit(solution)/shard_map/pallas_call | solution.py:141
  39.9 9.2 %shard_map.70.q_ref = bf16[3,256,256]{2,1,0:T(8,128)(2,1)S(1)} custom-call(bf16[256,256]{1,0:T(8,128)(2,1)S(1)} %get-tuple-element.5.sent.p_ref), custom_call_target="tpu_custom_call" | custom-call | tf_op jit(solution)/shard_map/pallas_call | solution.py:179
  49.1 7.8 %shard_map.71 = f32[256,256]{1,0:T(8,128)} custom-call(bf16[256,256]{1,0:T(8,128)(2,1)S(1)} %get-tuple-element.5.sent.p_ref, bf16[3,256,256]{2,1,0:T(8,128)(2,1)S(1)} %shard_map.70.q_ref), custom_call_target="tpu_custom_call" | custom-call | tf_op jit(solution)/shard_map/pallas_call | solution.py:141
Async XLA Ops:
  35.4 1.0 %copy-start = (bf16[2,256,256]{2,1,0:T(8,128)(2,1)S(1)}, bf16[2,256,256]{2,1,0:T(8,128)(2,1)}, u32[]{:S(2)}) copy-start(bf16[2,256,256]{2,1,0:T(8,128)(2,1)} %shard_map.68.rows_ref) | copy-start | bytes 786436

commit v9 on v8

--- a/solution.py
+++ b/solution.py
@@ -234,16 +234,17 @@
 
     barrier = pltpu.get_barrier_semaphore()
 
-    def greet_col(k, _):
-        pl.semaphore_signal(barrier, inc=1, device_id={"col": (j + k) % cols_n}, device_id_type=mesh_id)
-        return _
-
-    def greet_row(k, _):
+    def distance(d):
+        return min(d[0], 4 - d[0]) + min(d[1], 4 - d[1])
+
+    near_first = sorted(((dy, dz) for dy in range(4) for dz in range(4) if (dy, dz) != (0, 0)), key=distance)
+
+    for dy, dz in reversed(near_first):
+        peer = ((y0 + dy) % 4) * group + (z0 + dz) % group
+        pl.semaphore_signal(barrier, inc=1, device_id={"col": peer}, device_id_type=mesh_id)
+    rows_far_first = (4, 5, 3, 2, 6, 7, 1)
+    for k in rows_far_first:
         pl.semaphore_signal(barrier, inc=1, device_id={"row": (i + k) % rows_n}, device_id_type=mesh_id)
-        return _
-
-    lax.fori_loop(1, cols_n, greet_col, 0)
-    lax.fori_loop(1, rows_n, greet_row, 0)
 
     right_copy = pltpu.make_async_copy(right_hbm, right_buf, in_sem.at[4])
     leaf_copy = pltpu.make_async_copy(leaf_hbm, leaf_ref, in_sem.at[6])
@@ -294,11 +295,6 @@
     def turn(t):
         rows = slice(t * step_rows, (t + 1) * step_rows)
         left_t[:, rows] = left_buf[rows, :].T
-
-    def distance(d):
-        return min(d[0], 4 - d[0]) + min(d[1], 4 - d[1])
-
-    near_first = sorted(((dy, dz) for dy in range(4) for dz in range(4) if (dy, dz) != (0, 0)), key=distance)
 
     leaf_copy.wait()
     tree_copy.wait()
@@ -451,7 +447,8 @@
 
     lax.fori_loop(1, cols_n, f1_end, 0)
     f2s[...] = mm(to_rows, f1r[...].reshape(slots, width)).astype(BF16).reshape(f2s.shape)
-    lax.fori_loop(1, rows_n, f2_start, 0)
+    for k in rows_far_first:
+        f2_start(k, 0)
     forward_own = pltpu.make_async_copy(f2s.at[i], forward_part(i), in_sem.at[5])
     forward_own.start()
 

time: 57.1 us -> 56.5 us (0.989)
  Pallas kernels: 55.3 us -> 54.5 us
where the time goes in v9:
time: 56.5 us; the launch traced here: 56.1 us
  Pallas kernels  54.5 us (96%)
  local copies, waits for them, and re-layouts  0.94 us (2%)
  between operations  0.66 us (1%)
    pallas_call x1, Pallas kernels, sample_call(): pl.pallas_call(functools.partial(sample_kernel, rows_n, cols_n), out_shap...  34.4 us
    pallas_call x2, Pallas kernels, dense_call(): pl.pallas_call(kernel, out_shape=tuple((jax.ShapeDtypeStruct((width, widt...  10.9 us
    pallas_call x1, Pallas kernels, gather_call(): pl.pallas_call(gather_kernel, out_shape=jax.ShapeDtypeStruct((3, *sent.sh...  9.2 us

profile of v9, /device:TPU:1, one launch (start us, length us, event | category | flops | bytes accessed | tf_op | source)
XLA Modules:
  0.0 56.1 jit_solution(3385117873638224967)
XLA Ops:
  0.6 34.4 %shard_map.68.rows_ref = bf16[2,256,256]{2,1,0:T(8,128)(2,1)} custom-call(bf16[2048,1024]{1,0:T(8,128)(2,1)} %a_hbm.1, bf16[1024,256]{1,0:T(8,128)(2,1)} %right_hbm.1, bf16[2048,256]{1,0:T(8,128)(2,1)} %left_hbm.1, s32[128,128]{1,0:T(8,128)} %bitcast.5, s32[1,128]{1,0:T(1,128)} %bitcast.6), custom_call_target="tpu_custom_call" | custom-call | tf_op jit(solution)/shard_map/pallas_call | solution.py:472
  35.0 0.0 copy-start
  35.0 0.9 %copy-done = bf16[2,256,256]{2,1,0:T(8,128)(2,1)S(1)} copy-done((bf16[2,256,256]{2,1,0:T(8,128)(2,1)S(1)}, bf16[2,256,256]{2,1,0:T(8,128)(2,1)}, u32[]{:S(2)}) %copy-start) | copy-done | bytes 262168
  36.0 3.6 %shard_map.69 = (f32[256,256]{1,0:T(8,128)}, bf16[256,256]{1,0:T(8,128)(2,1)S(1)}) custom-call(bf16[2,256,256]{2,1,0:T(8,128)(2,1)S(1)} %copy-done), custom_call_target="tpu_custom_call" | custom-call | tf_op jit(solution)/shard_map/pallas_call | solution.py:141
  39.5 9.2 %shard_map.70.q_ref = bf16[3,256,256]{2,1,0:T(8,128)(2,1)S(1)} custom-call(bf16[256,256]{1,0:T(8,128)(2,1)S(1)} %get-tuple-element.5.sent.p_ref), custom_call_target="tpu_custom_call" | custom-call | tf_op jit(solution)/shard_map/pallas_call | solution.py:179
  48.7 7.4 %shard_map.71 = f32[256,256]{1,0:T(8,128)} custom-call(bf16[256,256]{1,0:T(8,128)(2,1)S(1)} %get-tuple-element.5.sent.p_ref, bf16[3,256,256]{2,1,0:T(8,128)(2,1)S(1)} %shard_map.70.q_ref), custom_call_target="tpu_custom_call" | custom-call | tf_op jit(solution)/shard_map/pallas_call | solution.py:141
Async XLA Ops:
  35.0 1.0 %copy-start = (bf16[2,256,256]{2,1,0:T(8,128)(2,1)S(1)}, bf16[2,256,256]{2,1,0:T(8,128)(2,1)}, u32[]{:S(2)}) copy-start(bf16[2,256,256]{2,1,0:T(8,128)(2,1)} %shard_map.68.rows_ref) | copy-start | bytes 786436
